TPU v7x, 512 devices: a whole 4x8x8 slice. The times are simulated.
512 devices in a mesh: cls: 128 (over y, z, core), dp: 4 (over x).
Axes of the slice: x: 4, y: 8, z: 8, core: 2. Of those that a mesh axis runs over, the one named last changes fastest.
Arguments:
- images: bfloat16 [65536, 4096], P(('cls', 'dp')), may hold values from -6 to 6
- defocus: bfloat16 [65536], P(('cls', 'dp')), may hold values from 0.5 to 2
- classes: int32 [65536, 1], P(('cls', 'dp')), may hold values from 0 to 127; in each aligned block of 128 rows (0 to 127, 128 to 255, ...) at most 2 rows name the same one
- rotations: int32 [65536], P(('cls', 'dp')), may hold values from 0 to 63
- references: bfloat16 [128, 64, 4096], P('cls'), may hold values from -6 to 6
Outputs:
- refined: bfloat16 [128, 64, 4096], P('cls', 'dp')
- misfit: float32 [65536], P(('cls', 'dp'))
Inputs may be any that keep to these rules, and one draw needn't show every extreme that they name: `classes`: among the rows of one device no class is named by more than 2 particles, and in every draw some device has exactly 2 particles of one class.
All inputs are finite; a program needn't handle non-finite values.
Results may differ from a plain program's by a relative error of at most 0.008.
Values may be sent and summed in bfloat16 or wider, within the bound.
No kernel may reach another device: no remote copies, remote signals or barrier semaphores. Data moves between devices by JAX's collectives and lax.ppermute only.
A program may use at most 64 MiB of HBM per device.

v0:
```python
import jax
import jax.numpy as jnp
from jax import lax
from jax.sharding import PartitionSpec as P

SIDE = 64


def wave_table(side_count):
    pixel_index = jnp.arange(side_count * side_count, dtype=jnp.int32)
    half_side = side_count // 2
    row_freq = (pixel_index // side_count + half_side) % side_count - half_side
    col_freq = (pixel_index % side_count + half_side) % side_count - half_side
    return (row_freq * row_freq + col_freq * col_freq).astype(jnp.float32) / float(
        half_side * half_side
    )


def contrast(defocus_rows, radius):
    phase = 20.0 * defocus_rows.astype(jnp.float32)[:, None] * radius[None, :] + 0.1
    return -jnp.sin(phase) * jnp.exp(-0.5 * radius)[None, :]


def sweep_rows(table, image_rows, rotation_rows, defocus_rows, radius):
    row_total = image_rows.shape[0]
    block_rows = min(64, row_total)
    block_count = row_total // block_rows
    rotation_count = table.shape[0]
    labels = jnp.arange(rotation_count, dtype=jnp.int32)

    def advance(gradient, block_index):
        row_start = block_index * block_rows
        image_block = lax.dynamic_slice_in_dim(image_rows, row_start, block_rows, 0)
        rotation_block = lax.dynamic_slice_in_dim(rotation_rows, row_start, block_rows, 0)
        defocus_block = lax.dynamic_slice_in_dim(defocus_rows, row_start, block_rows, 0)
        selector = (rotation_block[:, None] == labels[None, :]).astype(jnp.bfloat16)
        tiles = jnp.dot(selector, table, preferred_element_type=jnp.float32)
        contrast_rows = contrast(defocus_block, radius)
        residual = contrast_rows * tiles - image_block.astype(jnp.float32)
        misfit_rows = jnp.mean(residual * residual, axis=1)
        weighted = (contrast_rows * residual).astype(jnp.bfloat16)
        gradient = gradient + lax.dot_general(
            selector, weighted, (((0,), (0,)), ((), ())), preferred_element_type=jnp.float32
        )
        return (gradient, misfit_rows)

    start_grad = jnp.zeros((rotation_count, image_rows.shape[1]), jnp.float32)
    gradient, misfit_blocks = lax.scan(
        advance, start_grad, jnp.arange(block_count, dtype=jnp.int32)
    )
    return (gradient, misfit_blocks.reshape(row_total))


def build_slots(
    images, defocus, rotations, class_rows, class_rank, rank_first, slot_width, count_cls
):
    particle_ids = jnp.arange(images.shape[0], dtype=jnp.int32)
    inside = (class_rank >= rank_first) & (class_rank < rank_first + slot_width)
    slot_of = jnp.where(inside, class_rows * slot_width + class_rank - rank_first, -1)
    slot_ids = jnp.arange(count_cls * slot_width, dtype=jnp.int32)
    slot_match = slot_ids[:, None] == slot_of[None, :]
    slot_live = jnp.any(slot_match, axis=1)
    slot_source = jnp.sum(jnp.where(slot_match, particle_ids[None, :], 0), axis=1)
    send_images = jnp.where(
        slot_live[:, None], jnp.take(images, slot_source, axis=0), jnp.zeros((), jnp.bfloat16)
    )
    send_rotation = jnp.where(slot_live, jnp.take(rotations, slot_source), -1)
    send_defocus = jnp.where(
        slot_live, jnp.take(defocus, slot_source).astype(jnp.float32), 0.0
    ).astype(jnp.bfloat16)
    return (send_images, send_rotation, send_defocus)


def shards(images, defocus, classes, rotations, references):
    count_cls = lax.axis_size("cls")
    count_dp = lax.axis_size("dp")
    particle_count = images.shape[0]
    pixel_count = images.shape[1]
    rotation_count = references.shape[1]
    capacity = max(2, 2 * particle_count // count_cls)
    slot_count = count_cls * capacity
    radius = wave_table(SIDE)
    class_rows = classes[:, 0]
    particle_ids = jnp.arange(particle_count, dtype=jnp.int32)
    earlier_same = (class_rows[:, None] == class_rows[None, :]) & (
        particle_ids[None, :] < particle_ids[:, None]
    )
    class_rank = jnp.sum(earlier_same.astype(jnp.int32), axis=1)
    slot_of = class_rows * capacity + class_rank
    slot_ids = jnp.arange(slot_count, dtype=jnp.int32)
    slot_match = slot_ids[:, None] == slot_of[None, :]
    send_images, send_rotation, send_defocus = build_slots(
        images, defocus, rotations, class_rows, class_rank, 0, capacity, count_cls
    )
    recv_images, recv_rotation, recv_defocus = (
        lax.all_to_all(
            send_images.reshape(count_cls, capacity, pixel_count),
            "cls",
            split_axis=0,
            concat_axis=0,
            tiled=True,
        ),
        lax.all_to_all(
            send_rotation.astype(jnp.bfloat16).reshape(count_cls, capacity),
            "cls",
            split_axis=0,
            concat_axis=0,
            tiled=True,
        ),
        lax.all_to_all(
            send_defocus.reshape(count_cls, capacity),
            "cls",
            split_axis=0,
            concat_axis=0,
            tiled=True,
        ),
    )
    image_slots = recv_images.reshape(slot_count, pixel_count)
    rotation_slots = recv_rotation.reshape(slot_count).astype(jnp.int32)
    defocus_slots = recv_defocus.reshape(slot_count)
    labels = jnp.arange(rotation_count, dtype=jnp.int32)
    local_counts = jnp.sum((rotation_slots[:, None] == labels[None, :]).astype(jnp.float32), axis=0)
    counts = lax.psum(local_counts, "dp")
    damping = 0.5 * counts + 1.0
    table = references[0]
    grad_first, unused_first = sweep_rows(table, image_slots, rotation_slots, defocus_slots, radius)
    share_rows = rotation_count // count_dp
    share_start = lax.axis_index("dp") * share_rows
    damping_share = lax.dynamic_slice_in_dim(damping, share_start, share_rows, 0)
    grad_summed = lax.psum(grad_first.astype(jnp.bfloat16), "dp").astype(jnp.float32)
    table_next = (table.astype(jnp.float32) - grad_summed / damping[:, None]).astype(jnp.bfloat16)
    grad_second, misfit_slots = sweep_rows(
        table_next, image_slots, rotation_slots, defocus_slots, radius
    )
    second_share = lax.psum_scatter(
        grad_second.astype(jnp.bfloat16), "dp", scatter_dimension=0, tiled=True
    ).astype(jnp.float32)
    anchor_next = lax.dynamic_slice_in_dim(table_next, share_start, share_rows, 0).astype(
        jnp.float32
    )
    refined = (anchor_next - second_share / damping_share[:, None]).astype(jnp.bfloat16)
    returned = lax.all_to_all(
        misfit_slots.reshape(count_cls, capacity), "cls", split_axis=0, concat_axis=0, tiled=True
    )
    returned_slots = returned.reshape(slot_count)
    misfit = jnp.sum(jnp.where(slot_match, returned_slots[:, None], 0.0), axis=0)
    return (refined.reshape(1, share_rows, pixel_count), misfit)


def solution(mesh):
    in_specs = (
        P(("cls", "dp"), None),
        P(("cls", "dp")),
        P(("cls", "dp"), None),
        P(("cls", "dp")),
        P("cls", None, None),
    )
    out_specs = (P("cls", "dp", None), P(("cls", "dp")))
    return jax.shard_map(shards, mesh=mesh, in_specs=in_specs, out_specs=out_specs, check_vma=False)
```

profile of v0, /device:TPU:1, one launch (start us, length us, event | category | flops | bytes accessed | tf_op | source)
XLA Modules:
  0.0 286.1 jit_solution(12018576768820509236)
XLA Ops:
  12.4 18.4 %all-to-all-start = ((bf16[128,1,2]{2,1,0:T(2,128)(2,1)}), bf16[128,1,2]{2,1,0:T(2,128)(2,1)S(1)}, u32[]{:S(2)}, u32[]{:S(2)}) async-start(bf16[128,1,2]{2,1,0:T(2,128)(2,1)} %copy.18), calls=%async_computation | async-start | bytes 131072 | tf_op jit(solution)/shard_map/all_to_all | solution.py:103
  42.4 10.0 %all-to-all-start.1 = ((bf16[128,1,2]{2,1,0:T(2,128)(2,1)}), bf16[128,1,2]{2,1,0:T(2,128)(2,1)S(1)}, u32[]{:S(2)}, u32[]{:S(2)}) async-start(bf16[128,1,2]{2,1,0:T(2,128)(2,1)} %copy.21), calls=%async_computation.1 | async-start | bytes 131072 | tf_op jit(solution)/shard_map/all_to_all | solution.py:110
  52.4 5.4 %broadcast_select_fusion.1 = bf16[128,2,4096]{2,1,0:T(2,128)(2,1)} fusion(pred[128,2]{1,0:T(8,128)(4,1)S(1)} %broadcast_in_dim.108, bf16[128,2,4096]{2,1,0:T(2,128)(2,1)} %gather.23, pred[128,2]{1,0:T(8,128)(4,1)S(1)} %compare_and_fusion), kind=kLoop, calls=%fused_computation.103 | loop fusion | flops 2097152 | bytes 4194816 | tf_op jit(solution)/shard_map/jit(_where)/select_n | solution.py:64
  57.8 6.2 %all-to-all-done.1 = bf16[128,1,2]{2,1,0:T(2,128)(2,1)S(1)} async-done(((bf16[128,1,2]{2,1,0:T(2,128)(2,1)}), bf16[128,1,2]{2,1,0:T(2,128)(2,1)S(1)}, u32[]{:S(2)}, u32[]{:S(2)}) %all-to-all-start.1) | async-done | bytes 544 | tf_op jit(solution)/shard_map/all_to_all | solution.py:110
  64.0 8.0 %all-to-all-start.2 = ((bf16[128,2,4096]{2,1,0:T(2,128)(2,1)}), bf16[128,2,4096]{2,1,0:T(2,128)(2,1)}, u32[]{:S(2)}, u32[]{:S(2)}) async-start(bf16[128,2,4096]{2,1,0:T(2,128)(2,1)} %broadcast_select_fusion.1), calls=%async_computation.2 | async-start | bytes 4194304 | tf_op jit(solution)/shard_map/all_to_all | solution.py:96
  72.9 50.8 %all-to-all-done.2 = bf16[128,2,4096]{2,1,0:T(2,128)(2,1)} async-done(((bf16[128,2,4096]{2,1,0:T(2,128)(2,1)}), bf16[128,2,4096]{2,1,0:T(2,128)(2,1)}, u32[]{:S(2)}, u32[]{:S(2)}) %all-to-all-start.2) | async-done | bytes 2097184 | tf_op jit(solution)/shard_map/all_to_all | solution.py:96
  123.7 4.1 %reshape.220 = bf16[256,4096]{1,0:T(8,128)(2,1)} reshape(bf16[128,2,4096]{2,1,0:T(2,128)(2,1)} %all-to-all-done.2) | data formatting | bytes 4194304 | tf_op jit(solution)/shard_map/reshape | solution.py:118
  127.9 26.6 %while.26 = (s32[]{:T(128)}, f32[64,4096]{1,0:T(8,128)S(1)}, s32[4]{0:T(128)S(1)}, s32[256]{0:T(256)S(1)}, bf16[256]{0:T(256)(128)(2,1)S(1)}, /*index=5*/bf16[64...) while((s32[]{:T(128)}, f32[64,4096]{1,0:T(8,128)S(1)}, ...), condition=%wide.region_4.5_spmd.clone.clone, body=%wide.region_3.4_spmd.clone.clone.sunk | while | flops 70181000 | bytes 3213917 | solution.py:48
  129.3 5.2 %convolution_add_fusion.4 = f32[64,4096]{1,0:T(8,128)S(1)} fusion(bf16[64,4096]{1,0:T(8,128)(2,1)S(1)} %get-tuple-element.389, f32[64,4096]{1,0:T(8,128)S(1)} %get-tuple-element.372, bf16[256,4096]{1,0:T(8,128)(2,1)} %get-tuple-element.390, s32[]{:T(128)S(6)} %select_n.653, f32[4096]{0:T(1024)S(1)} %get-tuple-element.344, ...), kind=kOutput, calls=%fused_computation.7.clone.1 | convolution fusion | flops 70000640 | bytes 3180037 | tf_op jit(solution)/shard_map/while/body/eval_jaxpr/dot_general | solution.py:42
  135.9 5.2 %convolution_add_fusion.4 = f32[64,4096]{1,0:T(8,128)S(1)} fusion(bf16[64,4096]{1,0:T(8,128)(2,1)S(1)} %get-tuple-element.389, f32[64,4096]{1,0:T(8,128)S(1)} %get-tuple-element.372, bf16[256,4096]{1,0:T(8,128)(2,1)} %get-tuple-element.390, s32[]{:T(128)S(6)} %select_n.653, f32[4096]{0:T(1024)S(1)} %get-tuple-element.344, ...), kind=kOutput, calls=%fused_computation.7.clone.1 | convolution fusion | flops 70000640 | bytes 3180037 | tf_op jit(solution)/shard_map/while/body/eval_jaxpr/dot_general | solution.py:42
  142.6 5.2 %convolution_add_fusion.4 = f32[64,4096]{1,0:T(8,128)S(1)} fusion(bf16[64,4096]{1,0:T(8,128)(2,1)S(1)} %get-tuple-element.389, f32[64,4096]{1,0:T(8,128)S(1)} %get-tuple-element.372, bf16[256,4096]{1,0:T(8,128)(2,1)} %get-tuple-element.390, s32[]{:T(128)S(6)} %select_n.653, f32[4096]{0:T(1024)S(1)} %get-tuple-element.344, ...), kind=kOutput, calls=%fused_computation.7.clone.1 | convolution fusion | flops 70000640 | bytes 3180037 | tf_op jit(solution)/shard_map/while/body/eval_jaxpr/dot_general | solution.py:42
  149.3 5.2 %convolution_add_fusion.4 = f32[64,4096]{1,0:T(8,128)S(1)} fusion(bf16[64,4096]{1,0:T(8,128)(2,1)S(1)} %get-tuple-element.389, f32[64,4096]{1,0:T(8,128)S(1)} %get-tuple-element.372, bf16[256,4096]{1,0:T(8,128)(2,1)} %get-tuple-element.390, s32[]{:T(128)S(6)} %select_n.653, f32[4096]{0:T(1024)S(1)} %get-tuple-element.344, ...), kind=kOutput, calls=%fused_computation.7.clone.1 | convolution fusion | flops 70000640 | bytes 3180037 | tf_op jit(solution)/shard_map/while/body/eval_jaxpr/dot_general | solution.py:42
  155.6 8.5 %psum.15 = f32[64]{0:T(128)S(1)} all-reduce(f32[64]{0:T(128)S(1)} %convert_reduce_fusion.1), channel_id=1, replica_groups=mesh['cls'=128,'dp'=4] {'dp'}, use_global_device_ids=true, to_apply=%region_7.8 | all-reduce | flops 64 | bytes 512 | tf_op jit(solution)/shard_map/psum | solution.py:123
  164.0 37.8 %all-reduce.2.cloned.1.call-done = bf16[64,4096]{1,0:T(8,128)(2,1)} async-done(((bf16[64,4096]{1,0:T(8,128)(2,1)}), bf16[64,4096]{1,0:T(8,128)(2,1)}) %all-reduce.2.cloned.1.call-update) | async-done | bytes 524304 | tf_op jit(solution)/shard_map/psum | solution.py:130
  203.9 41.9 %while.27 = (s32[]{:T(128)}, f32[64,4096]{1,0:T(8,128)S(1)}, f32[4,64]{1,0:T(4,128)S(1)}, s32[4]{0:T(128)S(1)}, s32[256]{0:T(256)S(1)}, /*index=5*/bf16[256]{0:T...) while((s32[]{:T(128)}, f32[64,4096]{1,0:T(8,128)S(1)}, ...), condition=%wide.region_10.11_spmd.clone.clone, body=%wide.region_8.10_spmd.clone.clone.sunk | while | flops 71753864 | bytes 5344617 | solution.py:48
  205.4 5.1 %multiply_reduce_fusion.2 = (f32[64]{0:T(128)S(1)}, f32[64,4096]{1,0:T(8,128)S(1)}) fusion(bf16[256,4096]{1,0:T(8,128)(2,1)} %get-tuple-element.432, s32[]{:T(128)S(6)} %select_n.658, bf16[64,4096]{1,0:T(8,128)(2,1)} %get-tuple-element.431, s32[64]{0:T(128)S(1)} %dynamic_slice.72, f32[4096]{0:T(1024)S(1)} %get-tuple-element.354, ...), kind=kOutput, calls=%fused_computation.60.clone.1 | convolution fusion | flops 35917760 | bytes 2130692 | tf_op jit(solution)/shard_map/while/body/eval_jaxpr/dot_general | solution.py:37
  210.5 3.9 %convolution_add_fusion.5 = f32[64,4096]{1,0:T(8,128)S(1)} fusion(f32[64,4096]{1,0:T(8,128)S(1)} %get-tuple-element.412, f32[64,4096]{1,0:T(8,128)S(1)} %get-tuple-element.356, f32[4096]{0:T(1024)S(1)} %get-tuple-element.354, f32[4096]{0:T(1024)S(1)} %get-tuple-element.355, f32[64]{0:T(128)S(1)} %convert_multiply_fusion.5, pred[]{:T(512)S(6)} %compare.12, ...), kind=kOutput, calls=%fused_computation.57.clone.1 | convolution fusion | flops 35655680 | bytes 3179009 | tf_op jit(solution)/shard_map/while/body/eval_jaxpr/dot_general | solution.py:42
  215.8 5.1 %multiply_reduce_fusion.2 = (f32[64]{0:T(128)S(1)}, f32[64,4096]{1,0:T(8,128)S(1)}) fusion(bf16[256,4096]{1,0:T(8,128)(2,1)} %get-tuple-element.432, s32[]{:T(128)S(6)} %select_n.658, bf16[64,4096]{1,0:T(8,128)(2,1)} %get-tuple-element.431, s32[64]{0:T(128)S(1)} %dynamic_slice.72, f32[4096]{0:T(1024)S(1)} %get-tuple-element.354, ...), kind=kOutput, calls=%fused_computation.60.clone.1 | convolution fusion | flops 35917760 | bytes 2130692 | tf_op jit(solution)/shard_map/while/body/eval_jaxpr/dot_general | solution.py:37
  220.9 3.9 %convolution_add_fusion.5 = f32[64,4096]{1,0:T(8,128)S(1)} fusion(f32[64,4096]{1,0:T(8,128)S(1)} %get-tuple-element.412, f32[64,4096]{1,0:T(8,128)S(1)} %get-tuple-element.356, f32[4096]{0:T(1024)S(1)} %get-tuple-element.354, f32[4096]{0:T(1024)S(1)} %get-tuple-element.355, f32[64]{0:T(128)S(1)} %convert_multiply_fusion.5, pred[]{:T(512)S(6)} %compare.12, ...), kind=kOutput, calls=%fused_computation.57.clone.1 | convolution fusion | flops 35655680 | bytes 3179009 | tf_op jit(solution)/shard_map/while/body/eval_jaxpr/dot_general | solution.py:42
  226.3 5.1 %multiply_reduce_fusion.2 = (f32[64]{0:T(128)S(1)}, f32[64,4096]{1,0:T(8,128)S(1)}) fusion(bf16[256,4096]{1,0:T(8,128)(2,1)} %get-tuple-element.432, s32[]{:T(128)S(6)} %select_n.658, bf16[64,4096]{1,0:T(8,128)(2,1)} %get-tuple-element.431, s32[64]{0:T(128)S(1)} %dynamic_slice.72, f32[4096]{0:T(1024)S(1)} %get-tuple-element.354, ...), kind=kOutput, calls=%fused_computation.60.clone.1 | convolution fusion | flops 35917760 | bytes 2130692 | tf_op jit(solution)/shard_map/while/body/eval_jaxpr/dot_general | solution.py:37
  231.4 3.9 %convolution_add_fusion.5 = f32[64,4096]{1,0:T(8,128)S(1)} fusion(f32[64,4096]{1,0:T(8,128)S(1)} %get-tuple-element.412, f32[64,4096]{1,0:T(8,128)S(1)} %get-tuple-element.356, f32[4096]{0:T(1024)S(1)} %get-tuple-element.354, f32[4096]{0:T(1024)S(1)} %get-tuple-element.355, f32[64]{0:T(128)S(1)} %convert_multiply_fusion.5, pred[]{:T(512)S(6)} %compare.12, ...), kind=kOutput, calls=%fused_computation.57.clone.1 | convolution fusion | flops 35655680 | bytes 3179009 | tf_op jit(solution)/shard_map/while/body/eval_jaxpr/dot_general | solution.py:42
  236.8 5.1 %multiply_reduce_fusion.2 = (f32[64]{0:T(128)S(1)}, f32[64,4096]{1,0:T(8,128)S(1)}) fusion(bf16[256,4096]{1,0:T(8,128)(2,1)} %get-tuple-element.432, s32[]{:T(128)S(6)} %select_n.658, bf16[64,4096]{1,0:T(8,128)(2,1)} %get-tuple-element.431, s32[64]{0:T(128)S(1)} %dynamic_slice.72, f32[4096]{0:T(1024)S(1)} %get-tuple-element.354, ...), kind=kOutput, calls=%fused_computation.60.clone.1 | convolution fusion | flops 35917760 | bytes 2130692 | tf_op jit(solution)/shard_map/while/body/eval_jaxpr/dot_general | solution.py:37
  247.4 16.5 %all-to-all-start.3 = ((f32[128,1,2]{2,1,0:T(1,128)}), f32[128,1,2]{2,1,0:T(1,128)S(1)}, u32[]{:S(2)}, u32[]{:S(2)}) async-start(f32[128,1,2]{2,1,0:T(1,128)} %bitcast.5), calls=%async_computation.4 | async-start | bytes 131072 | tf_op jit(solution)/shard_map/all_to_all | solution.py:142
  264.0 11.4 %all-to-all-done.3 = f32[128,1,2]{2,1,0:T(1,128)S(1)} async-done(((f32[128,1,2]{2,1,0:T(1,128)}), f32[128,1,2]{2,1,0:T(1,128)S(1)}, u32[]{:S(2)}, u32[]{:S(2)}) %all-to-all-start.3) | async-done | bytes 1056 | tf_op jit(solution)/shard_map/all_to_all | solution.py:142
  (97 shorter events, 36.3 us)
Async XLA Ops:
  7.2 27.0 %copy-start = (bf16[128,4096]{1,0:T(8,128)(2,1)S(1)}, bf16[128,4096]{1,0:T(8,128)(2,1)}, u32[]{:S(2)}) copy-start(bf16[128,4096]{1,0:T(8,128)(2,1)} %param.9) | copy-start | bytes 3145732
  12.4 29.9 %all-to-all-start = ((bf16[128,1,2]{2,1,0:T(2,128)(2,1)}), bf16[128,1,2]{2,1,0:T(2,128)(2,1)S(1)}, u32[]{:S(2)}, u32[]{:S(2)}) async-start(bf16[128,1,2]{2,1,0:T(2,128)(2,1)} %copy.18), calls=%async_computation | async-start | bytes 131072 | tf_op jit(solution)/shard_map/all_to_all | solution.py:103
  42.4 21.6 %all-to-all-start.1 = ((bf16[128,1,2]{2,1,0:T(2,128)(2,1)}), bf16[128,1,2]{2,1,0:T(2,128)(2,1)S(1)}, u32[]{:S(2)}, u32[]{:S(2)}) async-start(bf16[128,1,2]{2,1,0:T(2,128)(2,1)} %copy.21), calls=%async_computation.1 | async-start | bytes 131072 | tf_op jit(solution)/shard_map/all_to_all | solution.py:110
  64.0 59.8 %all-to-all-start.2 = ((bf16[128,2,4096]{2,1,0:T(2,128)(2,1)}), bf16[128,2,4096]{2,1,0:T(2,128)(2,1)}, u32[]{:S(2)}, u32[]{:S(2)}) async-start(bf16[128,2,4096]{2,1,0:T(2,128)(2,1)} %broadcast_select_fusion.1), calls=%async_computation.2 | async-start | bytes 4194304 | tf_op jit(solution)/shard_map/all_to_all | solution.py:96
  72.0 129.9 %all-reduce.2.cloned.1.call-start = ((), (), s32[]{:S(2)}) async-start(), calls=%async_computation.5 | async-start | bytes 1048576 | tf_op jit(solution)/shard_map/psum | solution.py:130
  72.9 55.0 %copy-start.1 = (bf16[1,64,4096]{2,1,0:T(8,128)(2,1)S(1)}, bf16[1,64,4096]{2,1,0:T(8,128)(2,1)}, u32[]{:S(2)}) copy-start(bf16[1,64,4096]{2,1,0:T(8,128)(2,1)} %param.13) | copy-start | bytes 1572868
  155.4 122.1 %reduce-scatter.2.cloned.1.call-start = ((), (), s32[]{:S(2)}) async-start(), calls=%async_computation.6 | async-start | bytes 655360 | tf_op jit(solution)/shard_map/reduce_scatter | solution.py:135
  247.4 28.0 %all-to-all-start.3 = ((f32[128,1,2]{2,1,0:T(1,128)}), f32[128,1,2]{2,1,0:T(1,128)S(1)}, u32[]{:S(2)}, u32[]{:S(2)}) async-start(f32[128,1,2]{2,1,0:T(1,128)} %bitcast.5), calls=%async_computation.4 | async-start | bytes 131072 | tf_op jit(solution)/shard_map/all_to_all | solution.py:142
Sparse Core Ops, SparseCore 0:
  155.5 46.3 all-reduce.1
  246.8 27.7 reduce-scatter.1
where the time goes:
time: 287 us; the launch traced here: 286 us
  waiting for transfers between devices  110 us (38%)
  matrix products  56.8 us (20%)
  starting transfers between devices  53.1 us (19%)
  local copies, waits for them, and re-layouts  22.4 us (8%)
  other arithmetic  15.5 us (5%)
  between operations  14.2 us (5%)
  blocking collectives  8.48 us (3%)
  loops' own time  5.48 us (2%)
    all_to_all x1, waiting for transfers between devices, shards(): lax.all_to_all(send_images.reshape(count_cls, capacity, pixel_count), 'cl...  50.8 us
    psum x1, waiting for transfers between devices, shards(): lax.psum(grad_first.astype(jnp.bfloat16), 'dp').astype(jnp.float32)  37.8 us
    dot_general x8, matrix products, advance(): lax.dot_general(selector, weighted, (((0,), (0,)), ((), ())), preferred_e...  36.5 us
    dot_general x4, matrix products, advance(): tiles = jnp.dot(selector, table, preferred_element_type=jnp.float32)  20.4 us
    all_to_all x1, starting transfers between devices, shards(): lax.all_to_all(send_rotation.astype(jnp.bfloat16).reshape(count_cls, capa...  18.4 us
    all_to_all x1, starting transfers between devices, shards(): lax.all_to_all(misfit_slots.reshape(count_cls, capacity), 'cls', split_ax...  16.5 us
    all_to_all x1, waiting for transfers between devices, shards(): lax.all_to_all(misfit_slots.reshape(count_cls, capacity), 'cls', split_ax...  11.4 us
    all_to_all x1, starting transfers between devices, shards(): lax.all_to_all(send_defocus.reshape(count_cls, capacity), 'cls', split_ax...  10 us
  transfers between devices with their start and end apart: 6, of which 5 were waited for; matrix products, arithmetic and copies ran while one was open for 6% of the time, Pallas kernels for 0%

commit v1 on v0

v1 whole, which is shorter than its diff:
```python
import jax
import jax.numpy as jnp
from jax import lax
from jax.experimental import pallas as pl
from jax.experimental.pallas import tpu as pltpu
from jax.sharding import PartitionSpec as P

SIDE = 64
LANES = 128
SLOTS = 2
SINE = (
    6.283185306487567,
    -41.34170192978513,
    81.60520943195752,
    -76.70366785399285,
    41.99999017747946,
    -14.337026382067323,
)
VMEM = pl.BlockSpec(memory_space=pltpu.VMEM)
SMEM = pl.BlockSpec(memory_space=pltpu.SMEM)


def column_of(row, count):
    return jnp.broadcast_to(row, (count, row.shape[1])).T


def pack_body(class_ref, rotation_ref, defocus_ref, image_ref, out_ref, key_ref, rows_ref):
    particles = image_ref.shape[0]
    tiles = image_ref.shape[1] // LANES
    groups = out_ref.shape[0] // (particles * SLOTS) - tiles
    quarter = tiles // groups
    block = SLOTS * (quarter + 1)
    class_row = jnp.broadcast_to(class_ref[...].astype(jnp.float32), (particles, particles))
    class_column = class_row.T
    down = lax.broadcasted_iota(jnp.int32, (particles, particles), 0)
    across = lax.broadcasted_iota(jnp.int32, (particles, particles), 1)
    earlier = jnp.where((class_column == class_row) & (down < across), 1.0, 0.0)
    rank = jnp.sum(earlier, axis=0, keepdims=True)
    key_ref[...] = class_ref[...] * SLOTS + rank.astype(jnp.int32)
    rotation_row = rotation_ref[...].astype(jnp.float32) + 1.0
    defocus_row = defocus_ref[...]
    for slot in range(SLOTS):
        chosen = jnp.where((class_row == down.astype(jnp.float32)) & (rank == slot), 1.0, 0.0)
        rotation_column = jnp.sum(chosen * rotation_row, axis=1, keepdims=True) - 1.0
        defocus_column = jnp.sum(chosen * defocus_row, axis=1, keepdims=True)
        meta = jnp.where(across < LANES // 2, rotation_column, defocus_column)
        chooser = chosen.astype(jnp.bfloat16)
        for group in range(groups):
            moved = jnp.dot(
                chooser,
                image_ref[:, group * quarter * LANES : (group + 1) * quarter * LANES],
                preferred_element_type=jnp.float32,
            )
            first = group * block + slot
            for tile in range(quarter):
                rows_ref[pl.ds(first + tile * SLOTS, particles, stride=groups * block), :] = moved[
                    :, tile * LANES : (tile + 1) * LANES
                ]
            rows_ref[pl.ds(first + quarter * SLOTS, particles, stride=groups * block), :] = meta
    out_ref[...] = rows_ref[...].astype(jnp.bfloat16)


def refine_body(
    recv_ref,
    table_ref,
    phase_ref,
    decay_ref,
    out_ref,
    rows_ref,
    contrast_ref,
    sums_ref,
    pick_ref,
    pick_down_ref,
    misfit_ref,
    table_next_ref,
):
    rotations = table_ref.shape[0]
    width = table_ref.shape[1]
    quarter = width // LANES
    block = SLOTS * (quarter + 1)
    sources = recv_ref.shape[0] // block
    particles = sources * SLOTS
    groups = out_ref.shape[0]
    share = rotations // groups
    step = 128
    per_slot = sources // step
    rows_ref[...] = recv_ref[...].astype(jnp.float32)
    labels = lax.broadcasted_iota(jnp.int32, (step, LANES), 1).astype(jnp.float32)

    def meta_of(index):
        slot, chunk = index // per_slot, index % per_slot
        start = chunk * (step * block) + quarter * SLOTS + slot
        return rows_ref[pl.ds(start, step, stride=block), :]

    def mark(index, counts):
        meta = meta_of(index)
        hit = jnp.where(jnp.broadcast_to(meta[:, :1], (step, LANES)) == labels, 1.0, 0.0)
        place = pl.multiple_of(index * step, step)
        pick_ref[pl.ds(place, step), :] = hit.astype(jnp.bfloat16)
        flipped = hit.T[:rotations]
        pick_down_ref[:, pl.ds(place, step)] = flipped.astype(jnp.bfloat16)
        return counts + jnp.sum(flipped, axis=1, keepdims=True)

    counts = lax.fori_loop(
        0, particles // step, mark, jnp.zeros((rotations, 1), jnp.float32)
    )
    damping = jnp.broadcast_to(0.5 * counts + 1.0, (rotations, LANES))

    def first_pass(index, carry):
        slot, chunk = index // per_slot, index % per_slot
        place = pl.multiple_of(index * step, step)
        start = chunk * (step * block) + slot
        meta = meta_of(index)
        defocus = jnp.broadcast_to(meta[:, LANES // 2 : LANES // 2 + 1], (step, LANES))
        tiles = jnp.dot(
            pick_ref[pl.ds(place, step), :rotations],
            table_ref[...],
            preferred_element_type=jnp.float32,
        )
        for tile in range(quarter):
            image = rows_ref[pl.ds(start + tile * SLOTS, step, stride=block), :]
            turn = defocus * phase_ref[tile : tile + 1, :] + (0.1 / 6.283185307179586 + 0.25)
            turn = 0.25 - jnp.abs(turn - jnp.round(turn))
            square = turn * turn
            wave = jnp.full_like(square, SINE[-1])
            for factor in SINE[-2::-1]:
                wave = wave * square + factor
            contrast = wave * turn * decay_ref[tile : tile + 1, :]
            residual = contrast * tiles[:, tile * LANES : (tile + 1) * LANES] - image
            contrast_ref[tile, pl.ds(place, step), :] = contrast
            sums_ref[pl.ds(place, step), tile * 256 : tile * 256 + 128] = (
                contrast * residual
            ).astype(jnp.bfloat16)
            sums_ref[pl.ds(place, step), tile * 256 + 128 : tile * 256 + 256] = (
                contrast * contrast
            ).astype(jnp.bfloat16)
        return carry

    lax.fori_loop(0, particles // step, first_pass, 0)
    for tile in range(quarter):
        summed = jnp.dot(
            pick_down_ref[...],
            sums_ref[:, tile * 256 : (tile + 1) * 256],
            preferred_element_type=jnp.float32,
        )
        gradient, weight = summed[:, :LANES], summed[:, LANES:]
        lanes = slice(tile * LANES, (tile + 1) * LANES)
        table = table_ref[:, lanes].astype(jnp.float32)
        table_next = (table - gradient / damping).astype(jnp.bfloat16)
        table_next_ref[:, lanes] = table_next
        table_next = table_next.astype(jnp.float32)
        gradient = gradient - weight * (table - table_next)
        refined = (table_next - gradient / damping).astype(jnp.bfloat16)
        for group in range(groups):
            out_ref[group, :share, lanes] = refined[group * share : (group + 1) * share]

    def second_pass(index, carry):
        slot, chunk = index // per_slot, index % per_slot
        place = pl.multiple_of(index * step, step)
        start = chunk * (step * block) + slot
        tiles = jnp.dot(
            pick_ref[pl.ds(place, step), :rotations],
            table_next_ref[...],
            preferred_element_type=jnp.float32,
        )
        total = jnp.zeros((step, LANES), jnp.float32)
        for tile in range(quarter):
            image = rows_ref[pl.ds(start + tile * SLOTS, step, stride=block), :]
            residual = (
                contrast_ref[tile, pl.ds(place, step), :]
                * tiles[:, tile * LANES : (tile + 1) * LANES]
                - image
            )
            total = total + residual * residual
        misfit_ref[pl.ds(place, step), :] = total
        return carry

    lax.fori_loop(0, particles // step, second_pass, 0)
    ones = jnp.full((8, LANES), 1.0 / (groups * width), jnp.float32)
    level = lax.broadcasted_iota(jnp.int32, (8, width), 0)
    for group in range(groups):
        mine = misfit_ref[pl.ds(group, particles // groups, stride=groups), :]
        mean = lax.dot_general(
            ones,
            mine,
            (((1,), (1,)), ((), ())),
            precision=lax.Precision.HIGHEST,
            preferred_element_type=jnp.float32,
        )
        high = mean.astype(jnp.bfloat16).astype(jnp.float32)
        mean = jnp.where(level[:, : mean.shape[1]] == 0, high, mean - high)
        out_ref[group, share:, : mean.shape[1]] = mean.astype(jnp.bfloat16)
        out_ref[group, share:, mean.shape[1] :] = jnp.zeros(
            (8, width - mean.shape[1]), jnp.bfloat16
        )


def spread_body(recv_ref, out_ref):
    share = recv_ref.shape[1] - 8
    homes = out_ref.shape[0] // SLOTS
    total = jnp.sum(recv_ref[:, share:, : SLOTS * homes].astype(jnp.float32), axis=0)
    total = total[0:1] + total[1:2]
    slot = lax.broadcasted_iota(jnp.int32, out_ref.shape, 0) % SLOTS
    out_ref[...] = jnp.where(slot == 0, total[:, :homes], total[:, homes:])


def join_body(recv_ref, out_ref):
    groups, share = recv_ref.shape[0], recv_ref.shape[1] - 8
    width = recv_ref.shape[2]
    for group in range(groups):
        out_ref[:, group * width : (group + 1) * width] = recv_ref[group, :share, :]


def settle_body(own_ref, recv_ref, key_ref, out_ref):
    rows, lanes = recv_ref.shape
    lane = lax.broadcasted_iota(jnp.int32, (rows, lanes), 1)
    mine = jnp.sum(
        jnp.where(lane == own_ref[0, 0], recv_ref[...], 0.0), axis=1, keepdims=True
    )
    places = lax.broadcasted_iota(jnp.int32, (rows, key_ref.shape[1]), 0)
    out_ref[...] = jnp.sum(jnp.where(places == key_ref[...], mine, 0.0), axis=0, keepdims=True)


def shards(images, defocus, classes, rotations, references):
    count_cls = lax.axis_size("cls")
    count_dp = lax.axis_size("dp")
    particles, pixels = images.shape
    rotation_count = references.shape[1]
    share = rotation_count // count_dp
    width = pixels // count_dp
    quarter = width // LANES
    block = SLOTS * (quarter + 1)
    message_rows = count_cls * count_dp * block
    sources = count_cls * count_dp
    packed, key_row = pl.pallas_call(
        pack_body,
        out_shape=(
            jax.ShapeDtypeStruct((message_rows, LANES), jnp.bfloat16),
            jax.ShapeDtypeStruct((1, particles), jnp.int32),
        ),
        in_specs=[VMEM] * 4,
        out_specs=(VMEM, VMEM),
        scratch_shapes=[pltpu.VMEM((message_rows, LANES), jnp.float32)],
        name="pack",
    )(
        classes.reshape(1, particles),
        rotations.reshape(1, particles),
        defocus.astype(jnp.float32).reshape(1, particles),
        images,
    )
    received = lax.all_to_all(
        packed.reshape(message_rows // SLOTS, SLOTS, LANES),
        ("cls", "dp"),
        split_axis=0,
        concat_axis=0,
        tiled=True,
    ).reshape(message_rows, LANES)
    group = lax.axis_index("dp")
    pixel = (
        lax.broadcasted_iota(jnp.int32, (quarter, LANES), 0) * LANES
        + lax.broadcasted_iota(jnp.int32, (quarter, LANES), 1)
        + group * width
    )
    row_freq = (pixel // SIDE + SIDE // 2) % SIDE - SIDE // 2
    col_freq = (pixel % SIDE + SIDE // 2) % SIDE - SIDE // 2
    radius = (row_freq * row_freq + col_freq * col_freq).astype(jnp.float32) / float(
        (SIDE // 2) ** 2
    )
    phase = radius * (20.0 / 6.283185307179586)
    decay = jnp.exp(-0.5 * radius)
    table = lax.dynamic_slice_in_dim(references[0], group * width, width, 1)
    spread = pl.pallas_call(
        refine_body,
        out_shape=jax.ShapeDtypeStruct((count_dp, share + 8, width), jnp.bfloat16),
        in_specs=[VMEM] * 4,
        out_specs=VMEM,
        scratch_shapes=[
            pltpu.VMEM((message_rows, LANES), jnp.float32),
            pltpu.VMEM((quarter, sources * SLOTS, LANES), jnp.float32),
            pltpu.VMEM((sources * SLOTS, quarter * 2 * LANES), jnp.bfloat16),
            pltpu.VMEM((sources * SLOTS, LANES), jnp.bfloat16),
            pltpu.VMEM((rotation_count, sources * SLOTS), jnp.bfloat16),
            pltpu.VMEM((sources * SLOTS, LANES), jnp.float32),
            pltpu.VMEM((rotation_count, width), jnp.bfloat16),
        ],
        name="refine",
    )(received, table, phase, decay)
    turned = lax.all_to_all(spread, "dp", split_axis=0, concat_axis=0, tiled=True)
    returning = pl.pallas_call(
        spread_body,
        out_shape=jax.ShapeDtypeStruct((count_cls * SLOTS, LANES), jnp.float32),
        in_specs=[VMEM],
        out_specs=VMEM,
        name="spread",
    )(turned)
    returned = lax.all_to_all(
        returning.reshape(count_cls * SLOTS, 1, LANES),
        "cls",
        split_axis=0,
        concat_axis=0,
        tiled=True,
    ).reshape(count_cls * SLOTS, LANES)
    refined = pl.pallas_call(
        join_body,
        out_shape=jax.ShapeDtypeStruct((share, pixels), jnp.bfloat16),
        in_specs=[VMEM],
        out_specs=VMEM,
        name="join",
    )(turned)
    misfit = pl.pallas_call(
        settle_body,
        out_shape=jax.ShapeDtypeStruct((1, particles), jnp.float32),
        in_specs=[SMEM, VMEM, VMEM],
        out_specs=VMEM,
        name="settle",
    )(lax.axis_index("cls").astype(jnp.int32).reshape(1, 1), returned, key_row)
    return (refined.reshape(1, share, pixels), misfit.reshape(particles))


def solution(mesh):
    in_specs = (
        P(("cls", "dp"), None),
        P(("cls", "dp")),
        P(("cls", "dp"), None),
        P(("cls", "dp")),
        P("cls", None, None),
    )
    out_specs = (P("cls", "dp", None), P(("cls", "dp")))
    return jax.shard_map(shards, mesh=mesh, in_specs=in_specs, out_specs=out_specs, check_vma=False)
```

time: 287 us -> 136 us (0.47)
  matrix products: 56.8 us -> 0 us
  waiting for transfers between devices: 110 us -> 68.5 us
  starting transfers between devices: 53.1 us -> 32 us
  Pallas kernels: 0 us -> 20.7 us
  local copies, waits for them, and re-layouts: 22.4 us -> 2.75 us
  other arithmetic: 15.5 us -> 1.92 us
  between operations: 14.2 us -> 0.69 us
  loops' own time: 5.48 us -> 0 us
    dot_general x12 -> x0, matrix products: 56.8 us -> none  [the longest x8 36.5 us: advance(): lax.dot_general(selector, weighted, (((0,), (0,)), ((), ())), preferred_e...]
    psum x1 -> x0, waiting for transfers between devices: 37.8 us -> none  [shards(): lax.psum(grad_first.astype(jnp.bfloat16), 'dp').astype(jnp.float32)]
    all_to_all x4 -> x2, starting transfers between devices: 52.9 us -> 32 us  [the longest x1 22.2 us: shards(): lax.all_to_all(packed.reshape(message_rows // SLOTS, SLOTS, LANES), ('cls...]
    pallas_call x0 -> x5, Pallas kernels: none -> 20.7 us  [the longest x1 11.9 us: shards(): pl.pallas_call(refine_body, out_shape=jax.ShapeDtypeStruct((count_dp, sha...]
    all_to_all x0 -> x1, blocking collectives: none -> 9.33 us  [shards(): lax.all_to_all(spread, 'dp', split_axis=0, concat_axis=0, tiled=True)]
    gather x8 -> x0, local copies, waits for them, and re-layouts: 8.75 us -> none  [the longest x2 4.51 us: build_slots(): jnp.take(images, slot_source, axis=0)]
    psum x1 -> x0, blocking collectives: 8.48 us -> none  [shards(): counts = lax.psum(local_counts, 'dp')]
    another operation x2 -> x0, loops' own time: 5.48 us -> none  [sweep_rows(): lax.scan(advance, start_grad, jnp.arange(block_count, dtype=jnp.int32))]
  transfers between devices with their start and end apart: 6 -> 2, of which waited for: 5 -> 2; matrix products, arithmetic and copies ran while one was open for 6% -> 1% of each run, Pallas kernels for 0% -> 1%
where the time goes in v1:
time: 136 us
  waiting for transfers between devices  68.5 us (50%)
  starting transfers between devices  32 us (24%)
  Pallas kernels  20.7 us (15%)
  blocking collectives  9.33 us (7%)
  local copies, waits for them, and re-layouts  2.75 us (2%)
  other arithmetic  1.92 us (1%)
    all_to_all x1, waiting for transfers between devices, shards(): lax.all_to_all(packed.reshape(message_rows // SLOTS, SLOTS, LANES), ('cls...  57.9 us
    all_to_all x1, starting transfers between devices, shards(): lax.all_to_all(packed.reshape(message_rows // SLOTS, SLOTS, LANES), ('cls...  22.2 us
    pallas_call x1, Pallas kernels, shards(): pl.pallas_call(refine_body, out_shape=jax.ShapeDtypeStruct((count_dp, sha...  11.9 us
    all_to_all x1, waiting for transfers between devices, shards(): lax.all_to_all(returning.reshape(count_cls * SLOTS, 1, LANES), 'cls', spl...  10.7 us
    all_to_all x1, starting transfers between devices, shards(): lax.all_to_all(returning.reshape(count_cls * SLOTS, 1, LANES), 'cls', spl...  9.87 us
    all_to_all x1, blocking collectives, shards(): lax.all_to_all(spread, 'dp', split_axis=0, concat_axis=0, tiled=True)  9.33 us
    pallas_call x1, Pallas kernels, shards(): pl.pallas_call(pack_body, out_shape=(jax.ShapeDtypeStruct((message_rows,...  4.07 us
  transfers between devices with their start and end apart: 2, of which 2 were waited for; matrix products, arithmetic and copies ran while one was open for 1% of the time, Pallas kernels for 1%

profile of v1, /device:TPU:1, one launch (start us, length us, event | category | flops | bytes accessed | tf_op | source)
XLA Modules:
  0.0 135.9 jit_solution(15168799413668884876)
XLA Ops:
  0.6 0.0 copy-start
  0.6 1.2 bitcast_convert_fusion.defocus_ref
  1.9 4.1 %pack.1 = (bf16[9216,128]{1,0:T(8,128)(2,1)}, s32[1,128]{1,0:T(1,128)}) custom-call(s32[1,128]{1,0:T(1,128)} %bitcast.21, s32[1,128]{1,0:T(1,128)} %bitcast.22, f32[1,128]{1,0:T(1,128)} %bitcast_convert_fusion.defocus_ref, bf16[128,4096]{1,0:T(8,128)(2,1)} %image_ref.1), custom_call_target="tpu_custom_call" | custom-call | tf_op jit(solution)/shard_map/pack/pallas_call | solution.py:235
  5.9 22.2 %all-to-all-start = ((bf16[4608,2,128]{2,1,0:T(2,128)(2,1)}), bf16[4608,2,128]{2,1,0:T(2,128)(2,1)S(1)}, u32[]{:S(2)}, u32[]{:S(2)}) async-start(bf16[4608,2,128]{2,1,0:T(2,128)(2,1)} %bitcast.17), calls=%async_computation | async-start | bytes 4718592 | tf_op jit(solution)/shard_map/all_to_all | solution.py:251
  28.1 0.0 copy-done
  28.1 0.7 dynamic-slice_bitcast_fusion.table_ref
  28.8 0.7 multiply_exponential_fusion
  29.5 57.9 %all-to-all-done = bf16[4608,2,128]{2,1,0:T(2,128)(2,1)S(1)} async-done(((bf16[4608,2,128]{2,1,0:T(2,128)(2,1)}), bf16[4608,2,128]{2,1,0:T(2,128)(2,1)S(1)}, u32[]{:S(2)}, u32[]{:S(2)}) %all-to-all-start) | async-done | bytes 2359328 | tf_op jit(solution)/shard_map/all_to_all | solution.py:251
  87.4 0.0 copy-start.1
  87.4 1.4 %copy-done.1 = bf16[4608,2,128]{2,1,0:T(2,128)(2,1)} copy-done((bf16[4608,2,128]{2,1,0:T(2,128)(2,1)}, bf16[4608,2,128]{2,1,0:T(2,128)(2,1)S(1)}, u32[]{:S(2)}) %copy-start.1) | copy-done | bytes 2359320
  88.8 11.9 %refine.1 = bf16[4,24,1024]{2,1,0:T(8,128)(2,1)} custom-call(bf16[9216,128]{1,0:T(8,128)(2,1)} %bitcast.16, bf16[64,1024]{1,0:T(8,128)(2,1)} %dynamic-slice_bitcast_fusion.table_ref, f32[8,128]{1,0:T(8,128)} %get-tuple-element.7.phase_ref, f32[8,128]{1,0:T(8,128)} %get-tuple-element.6.decay_ref), custom_call_target="tpu_custom_call" | custom-call | tf_op jit(solution)/shard_map/refine/pallas_call | solution.py:272
  100.7 9.3 %all_to_all.15.recv_ref = bf16[4,24,1024]{2,1,0:T(8,128)(2,1)} all-to-all(bf16[4,24,1024]{2,1,0:T(8,128)(2,1)} %refine.1), channel_id=1, replica_groups=mesh['cls'=128,'dp'=4] {'dp'}, dimensions={0} | all-to-all | bytes 393216 | tf_op jit(solution)/shard_map/all_to_all | solution.py:288
  110.0 1.6 %spread.1 = f32[256,128]{1,0:T(8,128)} custom-call(bf16[4,24,1024]{2,1,0:T(8,128)(2,1)} %all_to_all.15.recv_ref), custom_call_target="tpu_custom_call" | custom-call | tf_op jit(solution)/shard_map/spread/pallas_call | solution.py:289
  111.6 9.9 %all-to-all-start.2 = ((f32[256,1,128]{2,1,0:T(1,128)}), f32[256,1,128]{2,1,0:T(1,128)S(1)}, u32[]{:S(2)}, u32[]{:S(2)}) async-start(f32[256,1,128]{2,1,0:T(1,128)} %bitcast.19), calls=%async_computation.2 | async-start | bytes 262144 | tf_op jit(solution)/shard_map/all_to_all | solution.py:296
  121.5 1.6 %join.1 = bf16[16,4096]{1,0:T(8,128)(2,1)} custom-call(bf16[4,24,1024]{2,1,0:T(8,128)(2,1)} %all_to_all.15.recv_ref), custom_call_target="tpu_custom_call" | custom-call | tf_op jit(solution)/shard_map/join/pallas_call | solution.py:303
  123.1 10.7 %all-to-all-done.2 = f32[256,1,128]{2,1,0:T(1,128)S(1)} async-done(((f32[256,1,128]{2,1,0:T(1,128)}), f32[256,1,128]{2,1,0:T(1,128)S(1)}, u32[]{:S(2)}, u32[]{:S(2)}) %all-to-all-start.2) | async-done | bytes 131104 | tf_op jit(solution)/shard_map/all_to_all | solution.py:296
  133.8 0.0 copy-start.2
  133.8 0.6 copy-done.2
  134.4 1.5 %settle.1 = f32[1,128]{1,0:T(1,128)} custom-call(s32[1,1]{1,0:T(1,128)} %bitcast.7.own_ref, f32[256,128]{1,0:T(8,128)} %bitcast.18, s32[1,128]{1,0:T(1,128)} %get-tuple-element.5.key_ref), custom_call_target="tpu_custom_call" | custom-call | tf_op jit(solution)/shard_map/settle/pallas_call | solution.py:310
  (1 shorter events, 0.0 us)
Async XLA Ops:
  0.6 27.5 %copy-start = (bf16[1,64,4096]{2,1,0:T(8,128)(2,1)S(1)}, bf16[1,64,4096]{2,1,0:T(8,128)(2,1)}, u32[]{:S(2)}) copy-start(bf16[1,64,4096]{2,1,0:T(8,128)(2,1)} %param.9) | copy-start | bytes 1572868
  5.9 81.4 %all-to-all-start = ((bf16[4608,2,128]{2,1,0:T(2,128)(2,1)}), bf16[4608,2,128]{2,1,0:T(2,128)(2,1)S(1)}, u32[]{:S(2)}, u32[]{:S(2)}) async-start(bf16[4608,2,128]{2,1,0:T(2,128)(2,1)} %bitcast.17), calls=%async_computation | async-start | bytes 4718592 | tf_op jit(solution)/shard_map/all_to_all | solution.py:251
  87.4 1.4 %copy-start.1 = (bf16[4608,2,128]{2,1,0:T(2,128)(2,1)}, bf16[4608,2,128]{2,1,0:T(2,128)(2,1)S(1)}, u32[]{:S(2)}) copy-start(bf16[4608,2,128]{2,1,0:T(2,128)(2,1)S(1)} %all-to-all-done) | copy-start | bytes 7077892
  111.6 22.1 %all-to-all-start.2 = ((f32[256,1,128]{2,1,0:T(1,128)}), f32[256,1,128]{2,1,0:T(1,128)S(1)}, u32[]{:S(2)}, u32[]{:S(2)}) async-start(f32[256,1,128]{2,1,0:T(1,128)} %bitcast.19), calls=%async_computation.2 | async-start | bytes 262144 | tf_op jit(solution)/shard_map/all_to_all | solution.py:296
  133.8 0.7 copy-start.2

commit v2 on v1

--- a/solution.py
+++ b/solution.py
@@ -38,7 +38,7 @@
     rank = jnp.sum(earlier, axis=0, keepdims=True)
     key_ref[...] = class_ref[...] * SLOTS + rank.astype(jnp.int32)
     rotation_row = rotation_ref[...].astype(jnp.float32) + 1.0
-    defocus_row = defocus_ref[...]
+    defocus_row = defocus_ref[...].astype(jnp.float32)
     for slot in range(SLOTS):
         chosen = jnp.where((class_row == down.astype(jnp.float32)) & (rank == slot), 1.0, 0.0)
         rotation_column = jnp.sum(chosen * rotation_row, axis=1, keepdims=True) - 1.0
@@ -63,8 +63,7 @@
 def refine_body(
     recv_ref,
     table_ref,
-    phase_ref,
-    decay_ref,
+    wave_ref,
     out_ref,
     rows_ref,
     contrast_ref,
@@ -106,12 +105,27 @@
     )
     damping = jnp.broadcast_to(0.5 * counts + 1.0, (rotations, LANES))
 
+    lane = lax.broadcasted_iota(jnp.int32, (step, LANES), 1)
+    half = jnp.where(lane < LANES // 2, 0, 1)
+
+    def cosine(turn, decay):
+        turn = 0.25 - jnp.abs(turn - jnp.round(turn))
+        square = turn * turn
+        wave = jnp.full_like(square, SINE[-1])
+        for factor in SINE[-2::-1]:
+            wave = wave * square + factor
+        return wave * (turn * decay)
+
     def first_pass(index, carry):
         slot, chunk = index // per_slot, index % per_slot
         place = pl.multiple_of(index * step, step)
         start = chunk * (step * block) + slot
         meta = meta_of(index)
         defocus = jnp.broadcast_to(meta[:, LANES // 2 : LANES // 2 + 1], (step, LANES))
+        rows = cosine(defocus * wave_ref[0:1, :] + wave_ref[1:2, :], wave_ref[2:3, :])
+        turn = defocus * wave_ref[3:4, :]
+        columns = cosine(turn, wave_ref[4:5, :])
+        columns_shifted = cosine(turn - 0.25, wave_ref[4:5, :])
         tiles = jnp.dot(
             pick_ref[pl.ds(place, step), :rotations],
             table_ref[...],
@@ -119,13 +133,11 @@
         )
         for tile in range(quarter):
             image = rows_ref[pl.ds(start + tile * SLOTS, step, stride=block), :]
-            turn = defocus * phase_ref[tile : tile + 1, :] + (0.1 / 6.283185307179586 + 0.25)
-            turn = 0.25 - jnp.abs(turn - jnp.round(turn))
-            square = turn * turn
-            wave = jnp.full_like(square, SINE[-1])
-            for factor in SINE[-2::-1]:
-                wave = wave * square + factor
-            contrast = wave * turn * decay_ref[tile : tile + 1, :]
+            spot = half + 2 * tile
+            contrast = (
+                jnp.take_along_axis(rows, spot, axis=1) * columns
+                + jnp.take_along_axis(rows, spot + 2 * quarter, axis=1) * columns_shifted
+            )
             residual = contrast * tiles[:, tile * LANES : (tile + 1) * LANES] - image
             contrast_ref[tile, pl.ds(place, step), :] = contrast
             sums_ref[pl.ds(place, step), tile * 256 : tile * 256 + 128] = (
@@ -245,7 +257,7 @@
     )(
         classes.reshape(1, particles),
         rotations.reshape(1, particles),
-        defocus.astype(jnp.float32).reshape(1, particles),
+        defocus.reshape(1, particles),
         images,
     )
     received = lax.all_to_all(
@@ -256,23 +268,33 @@
         tiled=True,
     ).reshape(message_rows, LANES)
     group = lax.axis_index("dp")
-    pixel = (
-        lax.broadcasted_iota(jnp.int32, (quarter, LANES), 0) * LANES
-        + lax.broadcasted_iota(jnp.int32, (quarter, LANES), 1)
-        + group * width
-    )
-    row_freq = (pixel // SIDE + SIDE // 2) % SIDE - SIDE // 2
-    col_freq = (pixel % SIDE + SIDE // 2) % SIDE - SIDE // 2
-    radius = (row_freq * row_freq + col_freq * col_freq).astype(jnp.float32) / float(
-        (SIDE // 2) ** 2
-    )
-    phase = radius * (20.0 / 6.283185307179586)
-    decay = jnp.exp(-0.5 * radius)
+    lane = jnp.arange(LANES, dtype=jnp.int32)
+    rows_held = width // SIDE
+    row_index = lane % rows_held + group * rows_held
+    row_freq = (row_index + SIDE // 2) % SIDE - SIDE // 2
+    col_freq = (lane % SIDE + SIDE // 2) % SIDE - SIDE // 2
+    row_radius = (row_freq * row_freq).astype(jnp.float32) / float((SIDE // 2) ** 2)
+    col_radius = (col_freq * col_freq).astype(jnp.float32) / float((SIDE // 2) ** 2)
+    per_turn = 20.0 / 6.283185307179586
+    offset = 0.1 / 6.283185307179586 + 0.25
+    blank = jnp.zeros((LANES,), jnp.float32)
+    wave = jnp.stack(
+        [
+            row_radius * per_turn,
+            offset + jnp.where(lane < rows_held, 0.0, 0.25),
+            jnp.exp(-0.5 * row_radius),
+            col_radius * per_turn,
+            jnp.exp(-0.5 * col_radius),
+            blank,
+            blank,
+            blank,
+        ]
+    )
     table = lax.dynamic_slice_in_dim(references[0], group * width, width, 1)
     spread = pl.pallas_call(
         refine_body,
         out_shape=jax.ShapeDtypeStruct((count_dp, share + 8, width), jnp.bfloat16),
-        in_specs=[VMEM] * 4,
+        in_specs=[VMEM] * 3,
         out_specs=VMEM,
         scratch_shapes=[
             pltpu.VMEM((message_rows, LANES), jnp.float32),
@@ -283,14 +305,16 @@
             pltpu.VMEM((sources * SLOTS, LANES), jnp.float32),
             pltpu.VMEM((rotation_count, width), jnp.bfloat16),
         ],
+        compiler_params=pltpu.CompilerParams(vmem_limit_bytes=22 << 20),
         name="refine",
-    )(received, table, phase, decay)
+    )(received, table, wave)
     turned = lax.all_to_all(spread, "dp", split_axis=0, concat_axis=0, tiled=True)
     returning = pl.pallas_call(
         spread_body,
         out_shape=jax.ShapeDtypeStruct((count_cls * SLOTS, LANES), jnp.float32),
         in_specs=[VMEM],
         out_specs=VMEM,
+        compiler_params=pltpu.CompilerParams(vmem_limit_bytes=2 << 20),
         name="spread",
     )(turned)
     returned = lax.all_to_all(
@@ -305,6 +329,7 @@
         out_shape=jax.ShapeDtypeStruct((share, pixels), jnp.bfloat16),
         in_specs=[VMEM],
         out_specs=VMEM,
+        compiler_params=pltpu.CompilerParams(vmem_limit_bytes=2 << 20),
         name="join",
     )(turned)
     misfit = pl.pallas_call(
@@ -312,6 +337,7 @@
         out_shape=jax.ShapeDtypeStruct((1, particles), jnp.float32),
         in_specs=[SMEM, VMEM, VMEM],
         out_specs=VMEM,
+        compiler_params=pltpu.CompilerParams(vmem_limit_bytes=2 << 20),
         name="settle",
     )(lax.axis_index("cls").astype(jnp.int32).reshape(1, 1), returned, key_row)
     return (refined.reshape(1, share, pixels), misfit.reshape(particles))

time: 136 us -> 127 us (0.934)
  Pallas kernels: 20.7 us -> 15.7 us
  local copies, waits for them, and re-layouts: 2.75 us -> 0.07 us
  waiting for transfers between devices: 68.5 us -> 70.7 us
  other arithmetic: 1.92 us -> 0.04 us
  blocking collectives: 9.33 us -> 7.95 us
    pallas_call x1, Pallas kernels: 11.9 us -> 9.62 us  [shards(): pl.pallas_call(refine_body, out_shape=jax.ShapeDtypeStruct((count_dp, sha...]
    unnamed x6 -> x4, local copies, waits for them, and re-layouts: 2.08 us -> 0.02 us
    all_to_all x1, blocking collectives: 9.33 us -> 7.95 us  [shards(): lax.all_to_all(spread, 'dp', split_axis=0, concat_axis=0, tiled=True)]
  transfers between devices with their start and end apart: 2 -> 2, of which waited for: 2 -> 2; matrix products, arithmetic and copies ran while one was open for 1% -> 0% of each run, Pallas kernels for 1% -> 1%
where the time goes in v2:
time: 127 us
  waiting for transfers between devices  70.7 us (56%)
  starting transfers between devices  31.8 us (25%)
  Pallas kernels  15.7 us (12%)
  blocking collectives  7.95 us (6%)
    all_to_all x1, waiting for transfers between devices, shards(): lax.all_to_all(packed.reshape(message_rows // SLOTS, SLOTS, LANES), ('cls...  59.1 us
    all_to_all x1, starting transfers between devices, shards(): lax.all_to_all(packed.reshape(message_rows // SLOTS, SLOTS, LANES), ('cls...  22.2 us
    all_to_all x1, waiting for transfers between devices, shards(): lax.all_to_all(returning.reshape(count_cls * SLOTS, 1, LANES), 'cls', spl...  11.6 us
    pallas_call x1, Pallas kernels, shards(): pl.pallas_call(refine_body, out_shape=jax.ShapeDtypeStruct((count_dp, sha...  9.62 us
    all_to_all x1, starting transfers between devices, shards(): lax.all_to_all(returning.reshape(count_cls * SLOTS, 1, LANES), 'cls', spl...  9.59 us
    all_to_all x1, blocking collectives, shards(): lax.all_to_all(spread, 'dp', split_axis=0, concat_axis=0, tiled=True)  7.95 us
    pallas_call x1, Pallas kernels, shards(): pl.pallas_call(pack_body, out_shape=(jax.ShapeDtypeStruct((message_rows,...  4.12 us
  transfers between devices with their start and end apart: 2, of which 2 were waited for; matrix products, arithmetic and copies ran while one was open for 0% of the time, Pallas kernels for 1%

profile of v2, /device:TPU:1, one launch (start us, length us, event | category | flops | bytes accessed | tf_op | source)
XLA Modules:
  0.0 127.0 jit_solution(9159932182684893055)
XLA Ops:
  0.6 0.0 copy-start
  0.6 4.1 %pack.1 = (bf16[9216,128]{1,0:T(8,128)(2,1)}, s32[1,128]{1,0:T(1,128)}) custom-call(s32[1,128]{1,0:T(1,128)} %bitcast.18, s32[1,128]{1,0:T(1,128)} %bitcast.19, bf16[1,128]{1,0:T(2,128)(2,1)} %bitcast.20, bf16[128,4096]{1,0:T(8,128)(2,1)} %image_ref.1), custom_call_target="tpu_custom_call" | custom-call | tf_op jit(solution)/shard_map/pack/pallas_call | solution.py:247
  4.8 22.2 %all-to-all-start = ((bf16[4608,2,128]{2,1,0:T(2,128)(2,1)}), bf16[4608,2,128]{2,1,0:T(2,128)(2,1)S(1)}, u32[]{:S(2)}, u32[]{:S(2)}) async-start(bf16[4608,2,128]{2,1,0:T(2,128)(2,1)} %bitcast.16), calls=%async_computation | async-start | bytes 4718592 | tf_op jit(solution)/shard_map/all_to_all | solution.py:263
  26.9 0.0 copy-start.1
  27.1 0.0 copy-done
  27.1 59.1 %all-to-all-done = bf16[4608,2,128]{2,1,0:T(2,128)(2,1)S(1)} async-done(((bf16[4608,2,128]{2,1,0:T(2,128)(2,1)}), bf16[4608,2,128]{2,1,0:T(2,128)(2,1)S(1)}, u32[]{:S(2)}, u32[]{:S(2)}) %all-to-all-start) | async-done | bytes 2359328 | tf_op jit(solution)/shard_map/all_to_all | solution.py:263
  86.2 9.6 %refine.1 = bf16[4,24,1024]{2,1,0:T(8,128)(2,1)S(1)} custom-call(bf16[9216,128]{1,0:T(8,128)(2,1)S(1)} %bitcast.14, bf16[64,1024]{1,0:T(8,128)(2,1)S(1)} %dynamic-slice_bitcast_fusion.table_ref, f32[8,128]{1,0:T(8,128)S(1)} %stack.5.wave_ref), custom_call_target="tpu_custom_call" | custom-call | tf_op jit(solution)/shard_map/refine/pallas_call | solution.py:294
  95.8 8.0 %all_to_all.15.recv_ref = bf16[4,24,1024]{2,1,0:T(8,128)(2,1)S(1)} all-to-all(bf16[4,24,1024]{2,1,0:T(8,128)(2,1)S(1)} %refine.1), channel_id=1, replica_groups=mesh['cls'=128,'dp'=4] {'dp'}, dimensions={0} | all-to-all | bytes 393216 | tf_op jit(solution)/shard_map/all_to_all | solution.py:311
  103.8 0.7 spread.1
  104.5 9.6 %all-to-all-start.2 = ((f32[256,1,128]{2,1,0:T(1,128)}), f32[256,1,128]{2,1,0:T(1,128)S(1)}, u32[]{:S(2)}, u32[]{:S(2)}) async-start(f32[256,1,128]{2,1,0:T(1,128)} %bitcast.9), calls=%async_computation.2 | async-start | bytes 262144 | tf_op jit(solution)/shard_map/all_to_all | solution.py:320
  114.1 0.7 join.1
  114.7 11.6 %all-to-all-done.2 = f32[256,1,128]{2,1,0:T(1,128)S(1)} async-done(((f32[256,1,128]{2,1,0:T(1,128)}), f32[256,1,128]{2,1,0:T(1,128)S(1)}, u32[]{:S(2)}, u32[]{:S(2)}) %all-to-all-start.2) | async-done | bytes 131104 | tf_op jit(solution)/shard_map/all_to_all | solution.py:320
  126.3 0.0 copy-done.1
  126.3 0.6 settle.1
  (7 shorter events, 0.1 us)
Async XLA Ops:
  0.6 26.4 %copy-start = (bf16[1,64,4096]{2,1,0:T(8,128)(2,1)S(1)}, bf16[1,64,4096]{2,1,0:T(8,128)(2,1)}, u32[]{:S(2)}) copy-start(bf16[1,64,4096]{2,1,0:T(8,128)(2,1)} %param.9) | copy-start | bytes 1572868
  4.8 81.5 %all-to-all-start = ((bf16[4608,2,128]{2,1,0:T(2,128)(2,1)}), bf16[4608,2,128]{2,1,0:T(2,128)(2,1)S(1)}, u32[]{:S(2)}, u32[]{:S(2)}) async-start(bf16[4608,2,128]{2,1,0:T(2,128)(2,1)} %bitcast.16), calls=%async_computation | async-start | bytes 4718592 | tf_op jit(solution)/shard_map/all_to_all | solution.py:263
  26.9 99.4 %copy-start.1 = (s32[1,128]{1,0:T(1,128)S(1)}, s32[1,128]{1,0:T(1,128)}, u32[]{:S(2)}) copy-start(s32[1,128]{1,0:T(1,128)} %get-tuple-element.5.key_ref) | copy-start | bytes 1540
  104.5 21.9 %all-to-all-start.2 = ((f32[256,1,128]{2,1,0:T(1,128)}), f32[256,1,128]{2,1,0:T(1,128)S(1)}, u32[]{:S(2)}, u32[]{:S(2)}) async-start(f32[256,1,128]{2,1,0:T(1,128)} %bitcast.9), calls=%async_computation.2 | async-start | bytes 262144 | tf_op jit(solution)/shard_map/all_to_all | solution.py:320

commit v3 on v2

--- a/solution.py
+++ b/solution.py
@@ -8,6 +8,7 @@
 SIDE = 64
 LANES = 128
 SLOTS = 2
+PARTS = 8
 SINE = (
     6.283185306487567,
     -41.34170192978513,
@@ -17,6 +18,7 @@
     -14.337026382067323,
 )
 VMEM = pl.BlockSpec(memory_space=pltpu.VMEM)
+ANY = pl.BlockSpec(memory_space=pl.ANY)
 SMEM = pl.BlockSpec(memory_space=pltpu.SMEM)
 
 
@@ -24,12 +26,40 @@
     return jnp.broadcast_to(row, (count, row.shape[1])).T
 
 
-def pack_body(class_ref, rotation_ref, defocus_ref, image_ref, out_ref, key_ref, rows_ref):
+def pack_body(
+    class_ref,
+    rotation_ref,
+    defocus_ref,
+    image_hbm,
+    out_hbm,
+    key_ref,
+    image_ref,
+    rows_ref,
+    out_ref,
+    load_sems,
+    store_sems,
+):
     particles = image_ref.shape[0]
     tiles = image_ref.shape[1] // LANES
     groups = out_ref.shape[0] // (particles * SLOTS) - tiles
     quarter = tiles // groups
+    width = quarter * LANES
     block = SLOTS * (quarter + 1)
+
+    def load(group):
+        columns = pl.ds(group * width, width)
+        return pltpu.make_async_copy(
+            image_hbm.at[:, columns], image_ref.at[:, columns], load_sems.at[group]
+        )
+
+    def store(part):
+        rows = pl.ds(part * part_rows, part_rows)
+        return pltpu.make_async_copy(out_ref.at[rows], out_hbm.at[rows], store_sems.at[part])
+
+    parts = store_sems.shape[0]
+    part_rows = out_ref.shape[0] // parts
+    for group in range(groups):
+        load(group).start()
     class_row = jnp.broadcast_to(class_ref[...].astype(jnp.float32), (particles, particles))
     class_column = class_row.T
     down = lax.broadcasted_iota(jnp.int32, (particles, particles), 0)
@@ -39,16 +69,23 @@
     key_ref[...] = class_ref[...] * SLOTS + rank.astype(jnp.int32)
     rotation_row = rotation_ref[...].astype(jnp.float32) + 1.0
     defocus_row = defocus_ref[...].astype(jnp.float32)
+    choosers = []
     for slot in range(SLOTS):
         chosen = jnp.where((class_row == down.astype(jnp.float32)) & (rank == slot), 1.0, 0.0)
         rotation_column = jnp.sum(chosen * rotation_row, axis=1, keepdims=True) - 1.0
         defocus_column = jnp.sum(chosen * defocus_row, axis=1, keepdims=True)
         meta = jnp.where(across < LANES // 2, rotation_column, defocus_column)
-        chooser = chosen.astype(jnp.bfloat16)
         for group in range(groups):
+            first = group * block + slot
+            rows_ref[pl.ds(first + quarter * SLOTS, particles, stride=groups * block), :] = meta
+        choosers.append(chosen.astype(jnp.bfloat16))
+    for group in range(groups):
+        load(group).wait()
+    for group in range(groups):
+        for slot in range(SLOTS):
             moved = jnp.dot(
-                chooser,
-                image_ref[:, group * quarter * LANES : (group + 1) * quarter * LANES],
+                choosers[slot],
+                image_ref[:, group * width : (group + 1) * width],
                 preferred_element_type=jnp.float32,
             )
             first = group * block + slot
@@ -56,14 +93,19 @@
                 rows_ref[pl.ds(first + tile * SLOTS, particles, stride=groups * block), :] = moved[
                     :, tile * LANES : (tile + 1) * LANES
                 ]
-            rows_ref[pl.ds(first + quarter * SLOTS, particles, stride=groups * block), :] = meta
-    out_ref[...] = rows_ref[...].astype(jnp.bfloat16)
+    for part in range(parts):
+        rows = slice(part * part_rows, (part + 1) * part_rows)
+        out_ref[rows] = rows_ref[rows].astype(jnp.bfloat16)
+        store(part).start()
+    for part in range(parts):
+        store(part).wait()
 
 
 def refine_body(
     recv_ref,
     table_ref,
     wave_ref,
+    widen_ref,
     out_ref,
     rows_ref,
     contrast_ref,
@@ -81,32 +123,13 @@
     particles = sources * SLOTS
     groups = out_ref.shape[0]
     share = rotations // groups
+    homes = sources // groups
     step = 128
     per_slot = sources // step
     rows_ref[...] = recv_ref[...].astype(jnp.float32)
-    labels = lax.broadcasted_iota(jnp.int32, (step, LANES), 1).astype(jnp.float32)
-
-    def meta_of(index):
-        slot, chunk = index // per_slot, index % per_slot
-        start = chunk * (step * block) + quarter * SLOTS + slot
-        return rows_ref[pl.ds(start, step, stride=block), :]
-
-    def mark(index, counts):
-        meta = meta_of(index)
-        hit = jnp.where(jnp.broadcast_to(meta[:, :1], (step, LANES)) == labels, 1.0, 0.0)
-        place = pl.multiple_of(index * step, step)
-        pick_ref[pl.ds(place, step), :] = hit.astype(jnp.bfloat16)
-        flipped = hit.T[:rotations]
-        pick_down_ref[:, pl.ds(place, step)] = flipped.astype(jnp.bfloat16)
-        return counts + jnp.sum(flipped, axis=1, keepdims=True)
-
-    counts = lax.fori_loop(
-        0, particles // step, mark, jnp.zeros((rotations, 1), jnp.float32)
-    )
-    damping = jnp.broadcast_to(0.5 * counts + 1.0, (rotations, LANES))
-
     lane = lax.broadcasted_iota(jnp.int32, (step, LANES), 1)
-    half = jnp.where(lane < LANES // 2, 0, 1)
+    labels = lane.astype(jnp.float32)
+    held = 2 * SLOTS * quarter
 
     def cosine(turn, decay):
         turn = 0.25 - jnp.abs(turn - jnp.round(turn))
@@ -116,27 +139,40 @@
             wave = wave * square + factor
         return wave * (turn * decay)
 
-    def first_pass(index, carry):
+    def rounded(values):
+        return values.astype(jnp.bfloat16).astype(jnp.float32)
+
+    def first_pass(index, counts):
         slot, chunk = index // per_slot, index % per_slot
         place = pl.multiple_of(index * step, step)
         start = chunk * (step * block) + slot
-        meta = meta_of(index)
+        meta = rows_ref[pl.ds(start + quarter * SLOTS, step, stride=block), :]
+        hit = jnp.where(jnp.broadcast_to(meta[:, :1], (step, LANES)) == labels, 1.0, 0.0)
+        pick = hit.astype(jnp.bfloat16)
+        pick_ref[pl.ds(place, step), :] = pick
+        flipped = hit.T[:rotations]
+        pick_down_ref[:, pl.ds(place, step)] = flipped.astype(jnp.bfloat16)
         defocus = jnp.broadcast_to(meta[:, LANES // 2 : LANES // 2 + 1], (step, LANES))
         rows = cosine(defocus * wave_ref[0:1, :] + wave_ref[1:2, :], wave_ref[2:3, :])
-        turn = defocus * wave_ref[3:4, :]
-        columns = cosine(turn, wave_ref[4:5, :])
-        columns_shifted = cosine(turn - 0.25, wave_ref[4:5, :])
-        tiles = jnp.dot(
-            pick_ref[pl.ds(place, step), :rotations],
-            table_ref[...],
-            preferred_element_type=jnp.float32,
-        )
+        high = rounded(rows)
+        middle = rounded(rows - high)
+        low = rows - high - middle
+        rows = jnp.where(lane < held, high, jnp.where(lane < 2 * held, middle, low))
+        columns = cosine(defocus * wave_ref[3:4, :] + wave_ref[4:5, :], wave_ref[5:6, :])
+        turned = pltpu.roll(columns, LANES // 2, 1)
+        columns, columns_shifted = (
+            jnp.where(lane < LANES // 2, columns, turned),
+            jnp.where(lane < LANES // 2, turned, columns),
+        )
+        wide = jnp.dot(
+            rows.astype(jnp.bfloat16), widen_ref[...], preferred_element_type=jnp.float32
+        )
+        tiles = jnp.dot(pick[:, :rotations], table_ref[...], preferred_element_type=jnp.float32)
         for tile in range(quarter):
             image = rows_ref[pl.ds(start + tile * SLOTS, step, stride=block), :]
-            spot = half + 2 * tile
             contrast = (
-                jnp.take_along_axis(rows, spot, axis=1) * columns
-                + jnp.take_along_axis(rows, spot + 2 * quarter, axis=1) * columns_shifted
+                wide[:, tile * 256 : tile * 256 + 128] * columns
+                + wide[:, tile * 256 + 128 : tile * 256 + 256] * columns_shifted
             )
             residual = contrast * tiles[:, tile * LANES : (tile + 1) * LANES] - image
             contrast_ref[tile, pl.ds(place, step), :] = contrast
@@ -146,16 +182,22 @@
             sums_ref[pl.ds(place, step), tile * 256 + 128 : tile * 256 + 256] = (
                 contrast * contrast
             ).astype(jnp.bfloat16)
-        return carry
-
-    lax.fori_loop(0, particles // step, first_pass, 0)
+        return counts + jnp.sum(flipped, axis=1, keepdims=True)
+
+    counts = lax.fori_loop(
+        0, particles // step, first_pass, jnp.zeros((rotations, 1), jnp.float32), unroll=2
+    )
+    damping = jnp.broadcast_to(0.5 * counts + 1.0, (rotations, LANES))
     for tile in range(quarter):
-        summed = jnp.dot(
-            pick_down_ref[...],
-            sums_ref[:, tile * 256 : (tile + 1) * 256],
-            preferred_element_type=jnp.float32,
-        )
-        gradient, weight = summed[:, :LANES], summed[:, LANES:]
+        if tile % 2 == 0:
+            summed = jnp.dot(
+                pick_down_ref[...],
+                sums_ref[:, tile * 256 : (tile + 2) * 256],
+                preferred_element_type=jnp.float32,
+            )
+        spot = tile % 2 * 256
+        gradient = summed[:, spot : spot + LANES]
+        weight = summed[:, spot + LANES : spot + 256]
         lanes = slice(tile * LANES, (tile + 1) * LANES)
         table = table_ref[:, lanes].astype(jnp.float32)
         table_next = (table - gradient / damping).astype(jnp.bfloat16)
@@ -187,11 +229,21 @@
         misfit_ref[pl.ds(place, step), :] = total
         return carry
 
-    lax.fori_loop(0, particles // step, second_pass, 0)
+    lax.fori_loop(0, particles // step, second_pass, 0, unroll=2)
     ones = jnp.full((8, LANES), 1.0 / (groups * width), jnp.float32)
     level = lax.broadcasted_iota(jnp.int32, (8, width), 0)
     for group in range(groups):
-        mine = misfit_ref[pl.ds(group, particles // groups, stride=groups), :]
+        mine = jnp.concatenate(
+            [
+                misfit_ref[
+                    pl.ds(slot * sources + part * (sources // 2) + group, homes // 2, stride=groups),
+                    :,
+                ]
+                for part in range(2)
+                for slot in range(SLOTS)
+            ],
+            axis=0,
+        )
         mean = lax.dot_general(
             ones,
             mine,
@@ -209,11 +261,11 @@
 
 def spread_body(recv_ref, out_ref):
     share = recv_ref.shape[1] - 8
-    homes = out_ref.shape[0] // SLOTS
-    total = jnp.sum(recv_ref[:, share:, : SLOTS * homes].astype(jnp.float32), axis=0)
+    homes, lanes = out_ref.shape
+    total = jnp.sum(recv_ref[:, share:, : 2 * lanes].astype(jnp.float32), axis=0)
     total = total[0:1] + total[1:2]
-    slot = lax.broadcasted_iota(jnp.int32, out_ref.shape, 0) % SLOTS
-    out_ref[...] = jnp.where(slot == 0, total[:, :homes], total[:, homes:])
+    home = lax.broadcasted_iota(jnp.int32, out_ref.shape, 0)
+    out_ref[...] = jnp.where(home < homes // 2, total[:, :lanes], total[:, lanes:])
 
 
 def join_body(recv_ref, out_ref):
@@ -226,11 +278,17 @@
 def settle_body(own_ref, recv_ref, key_ref, out_ref):
     rows, lanes = recv_ref.shape
     lane = lax.broadcasted_iota(jnp.int32, (rows, lanes), 1)
-    mine = jnp.sum(
-        jnp.where(lane == own_ref[0, 0], recv_ref[...], 0.0), axis=1, keepdims=True
-    )
-    places = lax.broadcasted_iota(jnp.int32, (rows, key_ref.shape[1]), 0)
-    out_ref[...] = jnp.sum(jnp.where(places == key_ref[...], mine, 0.0), axis=0, keepdims=True)
+    place = lax.broadcasted_iota(jnp.int32, (rows, key_ref.shape[1]), 0)
+    own = lax.rem(own_ref[0, 0], rows // 2)
+    total = jnp.zeros((rows, key_ref.shape[1]), jnp.float32)
+    for slot in range(SLOTS):
+        mine = jnp.sum(
+            jnp.where(lane == own + slot * (rows // 2), recv_ref[...], 0.0),
+            axis=1,
+            keepdims=True,
+        )
+        total = total + jnp.where(place * SLOTS + slot == key_ref[...], mine, 0.0)
+    out_ref[...] = jnp.sum(total, axis=0, keepdims=True)
 
 
 def shards(images, defocus, classes, rotations, references):
@@ -250,9 +308,15 @@
             jax.ShapeDtypeStruct((message_rows, LANES), jnp.bfloat16),
             jax.ShapeDtypeStruct((1, particles), jnp.int32),
         ),
-        in_specs=[VMEM] * 4,
-        out_specs=(VMEM, VMEM),
-        scratch_shapes=[pltpu.VMEM((message_rows, LANES), jnp.float32)],
+        in_specs=[VMEM, VMEM, VMEM, ANY],
+        out_specs=(ANY, VMEM),
+        scratch_shapes=[
+            pltpu.VMEM((particles, pixels), jnp.bfloat16),
+            pltpu.VMEM((message_rows, LANES), jnp.float32),
+            pltpu.VMEM((message_rows, LANES), jnp.bfloat16),
+            pltpu.SemaphoreType.DMA((count_dp,)),
+            pltpu.SemaphoreType.DMA((PARTS,)),
+        ],
         name="pack",
     )(
         classes.reshape(1, particles),
@@ -269,8 +333,8 @@
     ).reshape(message_rows, LANES)
     group = lax.axis_index("dp")
     lane = jnp.arange(LANES, dtype=jnp.int32)
-    rows_held = width // SIDE
-    row_index = lane % rows_held + group * rows_held
+    held = width // SIDE
+    row_index = lane % held + group * held
     row_freq = (row_index + SIDE // 2) % SIDE - SIDE // 2
     col_freq = (lane % SIDE + SIDE // 2) % SIDE - SIDE // 2
     row_radius = (row_freq * row_freq).astype(jnp.float32) / float((SIDE // 2) ** 2)
@@ -281,20 +345,24 @@
     wave = jnp.stack(
         [
             row_radius * per_turn,
-            offset + jnp.where(lane < rows_held, 0.0, 0.25),
+            offset + jnp.where(lane % (2 * held) < held, 0.0, 0.25),
             jnp.exp(-0.5 * row_radius),
             col_radius * per_turn,
+            jnp.where(lane < SIDE, 0.0, -0.25),
             jnp.exp(-0.5 * col_radius),
-            blank,
             blank,
             blank,
         ]
     )
+    source = lax.broadcasted_iota(jnp.int32, (LANES, 2 * width), 0)
+    target = lax.broadcasted_iota(jnp.int32, (LANES, 2 * width), 1)
+    wanted = target // LANES % 2 * held + target // (2 * LANES) * 2 + target % LANES // SIDE
+    widen = ((source % (2 * held) == wanted) & (source < 6 * held)).astype(jnp.bfloat16)
     table = lax.dynamic_slice_in_dim(references[0], group * width, width, 1)
     spread = pl.pallas_call(
         refine_body,
         out_shape=jax.ShapeDtypeStruct((count_dp, share + 8, width), jnp.bfloat16),
-        in_specs=[VMEM] * 3,
+        in_specs=[VMEM] * 4,
         out_specs=VMEM,
         scratch_shapes=[
             pltpu.VMEM((message_rows, LANES), jnp.float32),
@@ -307,23 +375,23 @@
         ],
         compiler_params=pltpu.CompilerParams(vmem_limit_bytes=22 << 20),
         name="refine",
-    )(received, table, wave)
+    )(received, table, wave, widen)
     turned = lax.all_to_all(spread, "dp", split_axis=0, concat_axis=0, tiled=True)
     returning = pl.pallas_call(
         spread_body,
-        out_shape=jax.ShapeDtypeStruct((count_cls * SLOTS, LANES), jnp.float32),
+        out_shape=jax.ShapeDtypeStruct((count_cls, LANES), jnp.float32),
         in_specs=[VMEM],
         out_specs=VMEM,
         compiler_params=pltpu.CompilerParams(vmem_limit_bytes=2 << 20),
         name="spread",
     )(turned)
     returned = lax.all_to_all(
-        returning.reshape(count_cls * SLOTS, 1, LANES),
+        returning.reshape(count_cls, 1, LANES),
         "cls",
         split_axis=0,
         concat_axis=0,
         tiled=True,
-    ).reshape(count_cls * SLOTS, LANES)
+    ).reshape(count_cls, LANES)
     refined = pl.pallas_call(
         join_body,
         out_shape=jax.ShapeDtypeStruct((share, pixels), jnp.bfloat16),

time: 127 us -> 124 us (0.976)
  Pallas kernels: 15.7 us -> 12.9 us
    pallas_call x1, Pallas kernels: 9.62 us -> 6.05 us  [shards(): pl.pallas_call(refine_body, out_shape=jax.ShapeDtypeStruct((count_dp, sha...]
where the time goes in v3:
time: 124 us; the launch traced here: 123 us
  waiting for transfers between devices  69.7 us (56%)
  starting transfers between devices  31.8 us (26%)
  Pallas kernels  12.9 us (10%)
  blocking collectives  7.95 us (6%)
    all_to_all x1, waiting for transfers between devices, shards(): lax.all_to_all(packed.reshape(message_rows // SLOTS, SLOTS, LANES), ('cls...  58.8 us
    all_to_all x1, starting transfers between devices, shards(): lax.all_to_all(packed.reshape(message_rows // SLOTS, SLOTS, LANES), ('cls...  22.2 us
    all_to_all x1, waiting for transfers between devices, shards(): lax.all_to_all(returning.reshape(count_cls, 1, LANES), 'cls', split_axis=...  10.9 us
    all_to_all x1, starting transfers between devices, shards(): lax.all_to_all(returning.reshape(count_cls, 1, LANES), 'cls', split_axis=...  9.59 us
    all_to_all x1, blocking collectives, shards(): lax.all_to_all(spread, 'dp', split_axis=0, concat_axis=0, tiled=True)  7.95 us
    pallas_call x1, Pallas kernels, shards(): pl.pallas_call(refine_body, out_shape=jax.ShapeDtypeStruct((count_dp, sha...  6.05 us
    pallas_call x1, Pallas kernels, shards(): pl.pallas_call(pack_body, out_shape=(jax.ShapeDtypeStruct((message_rows,...  4.93 us
  transfers between devices with their start and end apart: 2, of which 2 were waited for; matrix products, arithmetic and copies ran while one was open for 0% of the time, Pallas kernels for 1%

profile of v3, /device:TPU:1, one launch (start us, length us, event | category | flops | bytes accessed | tf_op | source)
XLA Modules:
  0.0 123.5 jit_solution(1784341313763240515)
XLA Ops:
  0.6 0.0 copy-start
  0.6 4.9 %pack.1 = (bf16[9216,128]{1,0:T(8,128)(2,1)}, s32[1,128]{1,0:T(1,128)}) custom-call(s32[1,128]{1,0:T(1,128)} %bitcast.18, s32[1,128]{1,0:T(1,128)} %bitcast.19, bf16[1,128]{1,0:T(2,128)(2,1)} %bitcast.20, bf16[128,4096]{1,0:T(8,128)(2,1)} %image_hbm.1), custom_call_target="tpu_custom_call" | custom-call | tf_op jit(solution)/shard_map/pack/pallas_call | solution.py:305
  5.6 22.2 %all-to-all-start = ((bf16[4608,2,128]{2,1,0:T(2,128)(2,1)}), bf16[4608,2,128]{2,1,0:T(2,128)(2,1)S(1)}, u32[]{:S(2)}, u32[]{:S(2)}) async-start(bf16[4608,2,128]{2,1,0:T(2,128)(2,1)} %bitcast.16), calls=%async_computation | async-start | bytes 4718592 | tf_op jit(solution)/shard_map/all_to_all | solution.py:327
  27.9 0.0 copy-done
  28.0 0.0 copy-start.1
  28.0 0.3 and_convert_fusion.widen_ref
  28.3 58.8 %all-to-all-done = bf16[4608,2,128]{2,1,0:T(2,128)(2,1)S(1)} async-done(((bf16[4608,2,128]{2,1,0:T(2,128)(2,1)}), bf16[4608,2,128]{2,1,0:T(2,128)(2,1)S(1)}, u32[]{:S(2)}, u32[]{:S(2)}) %all-to-all-start) | async-done | bytes 2359328 | tf_op jit(solution)/shard_map/all_to_all | solution.py:327
  87.0 6.1 %refine.1 = bf16[4,24,1024]{2,1,0:T(8,128)(2,1)S(1)} custom-call(bf16[9216,128]{1,0:T(8,128)(2,1)S(1)} %bitcast.14, bf16[64,1024]{1,0:T(8,128)(2,1)S(1)} %dynamic-slice_bitcast_fusion.table_ref, f32[8,128]{1,0:T(8,128)S(1)} %stack.5.wave_ref, bf16[128,2048]{1,0:T(8,128)(2,1)S(1)} %and_convert_fusion.widen_ref), custom_call_target="tpu_custom_call" | custom-call | tf_op jit(solution)/shard_map/refine/pallas_call | solution.py:362
  93.1 8.0 %all_to_all.15.recv_ref = bf16[4,24,1024]{2,1,0:T(8,128)(2,1)S(1)} all-to-all(bf16[4,24,1024]{2,1,0:T(8,128)(2,1)S(1)} %refine.1), channel_id=1, replica_groups=mesh['cls'=128,'dp'=4] {'dp'}, dimensions={0} | all-to-all | bytes 393216 | tf_op jit(solution)/shard_map/all_to_all | solution.py:379
  101.0 0.6 spread.1
  101.7 9.6 %all-to-all-start.2 = ((f32[128,1,128]{2,1,0:T(1,128)}), f32[128,1,128]{2,1,0:T(1,128)S(1)}, u32[]{:S(2)}, u32[]{:S(2)}) async-start(f32[128,1,128]{2,1,0:T(1,128)} %bitcast.9), calls=%async_computation.2 | async-start | bytes 131072 | tf_op jit(solution)/shard_map/all_to_all | solution.py:388
  111.3 0.7 join.1
  111.9 10.9 %all-to-all-done.2 = f32[128,1,128]{2,1,0:T(1,128)S(1)} async-done(((f32[128,1,128]{2,1,0:T(1,128)}), f32[128,1,128]{2,1,0:T(1,128)S(1)}, u32[]{:S(2)}, u32[]{:S(2)}) %all-to-all-start.2) | async-done | bytes 65568 | tf_op jit(solution)/shard_map/all_to_all | solution.py:388
  122.8 0.0 copy-done.1
  122.8 0.6 settle.1
  (13 shorter events, 0.1 us)
Async XLA Ops:
  0.6 27.3 %copy-start = (bf16[1,64,4096]{2,1,0:T(8,128)(2,1)S(1)}, bf16[1,64,4096]{2,1,0:T(8,128)(2,1)}, u32[]{:S(2)}) copy-start(bf16[1,64,4096]{2,1,0:T(8,128)(2,1)} %param.9) | copy-start | bytes 1572868
  5.6 81.4 %all-to-all-start = ((bf16[4608,2,128]{2,1,0:T(2,128)(2,1)}), bf16[4608,2,128]{2,1,0:T(2,128)(2,1)S(1)}, u32[]{:S(2)}, u32[]{:S(2)}) async-start(bf16[4608,2,128]{2,1,0:T(2,128)(2,1)} %bitcast.16), calls=%async_computation | async-start | bytes 4718592 | tf_op jit(solution)/shard_map/all_to_all | solution.py:327
  28.0 94.9 %copy-start.1 = (s32[1,128]{1,0:T(1,128)S(1)}, s32[1,128]{1,0:T(1,128)}, u32[]{:S(2)}) copy-start(s32[1,128]{1,0:T(1,128)} %get-tuple-element.5.key_ref) | copy-start | bytes 1540
  101.7 21.2 %all-to-all-start.2 = ((f32[128,1,128]{2,1,0:T(1,128)}), f32[128,1,128]{2,1,0:T(1,128)S(1)}, u32[]{:S(2)}, u32[]{:S(2)}) async-start(f32[128,1,128]{2,1,0:T(1,128)} %bitcast.9), calls=%async_computation.2 | async-start | bytes 131072 | tf_op jit(solution)/shard_map/all_to_all | solution.py:388

commit v4 on v3

--- a/solution.py
+++ b/solution.py
@@ -8,14 +8,13 @@
 SIDE = 64
 LANES = 128
 SLOTS = 2
-PARTS = 8
+PARTS = 2
 SINE = (
-    6.283185306487567,
-    -41.34170192978513,
-    81.60520943195752,
-    -76.70366785399285,
-    41.99999017747946,
-    -14.337026382067323,
+    6.283185160099087,
+    -41.341655032897165,
+    81.60100414087813,
+    -76.54978347470858,
+    39.53671300031621,
 )
 VMEM = pl.BlockSpec(memory_space=pltpu.VMEM)
 ANY = pl.BlockSpec(memory_space=pl.ANY)
@@ -30,13 +29,11 @@
     class_ref,
     rotation_ref,
     defocus_ref,
-    image_hbm,
+    image_ref,
     out_hbm,
     key_ref,
-    image_ref,
     rows_ref,
     out_ref,
-    load_sems,
     store_sems,
 ):
     particles = image_ref.shape[0]
@@ -46,20 +43,12 @@
     width = quarter * LANES
     block = SLOTS * (quarter + 1)
 
-    def load(group):
-        columns = pl.ds(group * width, width)
-        return pltpu.make_async_copy(
-            image_hbm.at[:, columns], image_ref.at[:, columns], load_sems.at[group]
-        )
-
     def store(part):
         rows = pl.ds(part * part_rows, part_rows)
         return pltpu.make_async_copy(out_ref.at[rows], out_hbm.at[rows], store_sems.at[part])
 
     parts = store_sems.shape[0]
     part_rows = out_ref.shape[0] // parts
-    for group in range(groups):
-        load(group).start()
     class_row = jnp.broadcast_to(class_ref[...].astype(jnp.float32), (particles, particles))
     class_column = class_row.T
     down = lax.broadcasted_iota(jnp.int32, (particles, particles), 0)
@@ -79,21 +68,20 @@
             first = group * block + slot
             rows_ref[pl.ds(first + quarter * SLOTS, particles, stride=groups * block), :] = meta
         choosers.append(chosen.astype(jnp.bfloat16))
-    for group in range(groups):
-        load(group).wait()
-    for group in range(groups):
-        for slot in range(SLOTS):
-            moved = jnp.dot(
-                choosers[slot],
-                image_ref[:, group * width : (group + 1) * width],
-                preferred_element_type=jnp.float32,
-            )
-            first = group * block + slot
-            for tile in range(quarter):
-                rows_ref[pl.ds(first + tile * SLOTS, particles, stride=groups * block), :] = moved[
-                    :, tile * LANES : (tile + 1) * LANES
-                ]
+    owners = particles // parts
     for part in range(parts):
+        for group in range(groups):
+            for slot in range(SLOTS):
+                moved = jnp.dot(
+                    choosers[slot][part * owners : (part + 1) * owners],
+                    image_ref[:, group * width : (group + 1) * width],
+                    preferred_element_type=jnp.float32,
+                )
+                first = part * part_rows + group * block + slot
+                for tile in range(quarter):
+                    rows_ref[pl.ds(first + tile * SLOTS, owners, stride=groups * block), :] = (
+                        moved[:, tile * LANES : (tile + 1) * LANES]
+                    )
         rows = slice(part * part_rows, (part + 1) * part_rows)
         out_ref[rows] = rows_ref[rows].astype(jnp.bfloat16)
         store(part).start()
@@ -126,7 +114,6 @@
     homes = sources // groups
     step = 128
     per_slot = sources // step
-    rows_ref[...] = recv_ref[...].astype(jnp.float32)
     lane = lax.broadcasted_iota(jnp.int32, (step, LANES), 1)
     labels = lane.astype(jnp.float32)
     held = 2 * SLOTS * quarter
@@ -142,9 +129,15 @@
     def rounded(values):
         return values.astype(jnp.bfloat16).astype(jnp.float32)
 
-    def first_pass(index, counts):
-        slot, chunk = index // per_slot, index % per_slot
-        place = pl.multiple_of(index * step, step)
+    def first_pass(chunk, counts):
+        held_rows = pl.ds(pl.multiple_of(chunk * (step * block), step), step * block)
+        rows_ref[held_rows, :] = recv_ref[held_rows, :].astype(jnp.float32)
+        for slot in range(SLOTS):
+            counts = counts + first_slot(chunk, slot)
+        return counts
+
+    def first_slot(chunk, slot):
+        place = pl.multiple_of(slot * sources + chunk * step, step)
         start = chunk * (step * block) + slot
         meta = rows_ref[pl.ds(start + quarter * SLOTS, step, stride=block), :]
         hit = jnp.where(jnp.broadcast_to(meta[:, :1], (step, LANES)) == labels, 1.0, 0.0)
@@ -182,11 +175,9 @@
             sums_ref[pl.ds(place, step), tile * 256 + 128 : tile * 256 + 256] = (
                 contrast * contrast
             ).astype(jnp.bfloat16)
-        return counts + jnp.sum(flipped, axis=1, keepdims=True)
-
-    counts = lax.fori_loop(
-        0, particles // step, first_pass, jnp.zeros((rotations, 1), jnp.float32), unroll=2
-    )
+        return jnp.sum(flipped, axis=1, keepdims=True)
+
+    counts = lax.fori_loop(0, per_slot, first_pass, jnp.zeros((rotations, 1), jnp.float32))
     damping = jnp.broadcast_to(0.5 * counts + 1.0, (rotations, LANES))
     for tile in range(quarter):
         if tile % 2 == 0:
@@ -308,13 +299,11 @@
             jax.ShapeDtypeStruct((message_rows, LANES), jnp.bfloat16),
             jax.ShapeDtypeStruct((1, particles), jnp.int32),
         ),
-        in_specs=[VMEM, VMEM, VMEM, ANY],
+        in_specs=[VMEM] * 4,
         out_specs=(ANY, VMEM),
         scratch_shapes=[
-            pltpu.VMEM((particles, pixels), jnp.bfloat16),
             pltpu.VMEM((message_rows, LANES), jnp.float32),
             pltpu.VMEM((message_rows, LANES), jnp.bfloat16),
-            pltpu.SemaphoreType.DMA((count_dp,)),
             pltpu.SemaphoreType.DMA((PARTS,)),
         ],
         name="pack",

time: 124 us -> 123 us (level)
  no operation moved by 1% of the time
where the time goes in v4:
time: 123 us
  waiting for transfers between devices  69.7 us (57%)
  starting transfers between devices  31.7 us (26%)
  Pallas kernels  12.2 us (10%)
  blocking collectives  7.96 us (6%)
    all_to_all x1, waiting for transfers between devices, shards(): lax.all_to_all(packed.reshape(message_rows // SLOTS, SLOTS, LANES), ('cls...  58.8 us
    all_to_all x1, starting transfers between devices, shards(): lax.all_to_all(packed.reshape(message_rows // SLOTS, SLOTS, LANES), ('cls...  22.1 us
    all_to_all x1, waiting for transfers between devices, shards(): lax.all_to_all(returning.reshape(count_cls, 1, LANES), 'cls', split_axis=...  10.9 us
    all_to_all x1, starting transfers between devices, shards(): lax.all_to_all(returning.reshape(count_cls, 1, LANES), 'cls', split_axis=...  9.58 us
    all_to_all x1, blocking collectives, shards(): lax.all_to_all(spread, 'dp', split_axis=0, concat_axis=0, tiled=True)  7.96 us
    pallas_call x1, Pallas kernels, shards(): pl.pallas_call(refine_body, out_shape=jax.ShapeDtypeStruct((count_dp, sha...  5.98 us
    pallas_call x1, Pallas kernels, shards(): pl.pallas_call(pack_body, out_shape=(jax.ShapeDtypeStruct((message_rows,...  4.28 us
  transfers between devices with their start and end apart: 2, of which 2 were waited for; matrix products, arithmetic and copies ran while one was open for 0% of the time, Pallas kernels for 1%

profile of v4, /device:TPU:1, one launch (start us, length us, event | category | flops | bytes accessed | tf_op | source)
XLA Modules:
  0.0 122.7 jit_solution(16111812581336945959)
XLA Ops:
  0.6 0.0 copy-start
  0.6 4.3 %pack.1 = (bf16[9216,128]{1,0:T(8,128)(2,1)}, s32[1,128]{1,0:T(1,128)}) custom-call(s32[1,128]{1,0:T(1,128)} %bitcast.18, s32[1,128]{1,0:T(1,128)} %bitcast.19, bf16[1,128]{1,0:T(2,128)(2,1)} %bitcast.20, bf16[128,4096]{1,0:T(8,128)(2,1)} %image_ref.1), custom_call_target="tpu_custom_call" | custom-call | tf_op jit(solution)/shard_map/pack/pallas_call | solution.py:296
  4.9 22.1 %all-to-all-start = ((bf16[4608,2,128]{2,1,0:T(2,128)(2,1)}), bf16[4608,2,128]{2,1,0:T(2,128)(2,1)S(1)}, u32[]{:S(2)}, u32[]{:S(2)}) async-start(bf16[4608,2,128]{2,1,0:T(2,128)(2,1)} %bitcast.16), calls=%async_computation | async-start | bytes 4718592 | tf_op jit(solution)/shard_map/all_to_all | solution.py:316
  27.3 0.0 copy-done
  27.3 0.0 copy-start.1
  27.3 0.3 and_convert_fusion.widen_ref
  27.6 58.8 %all-to-all-done = bf16[4608,2,128]{2,1,0:T(2,128)(2,1)S(1)} async-done(((bf16[4608,2,128]{2,1,0:T(2,128)(2,1)}), bf16[4608,2,128]{2,1,0:T(2,128)(2,1)S(1)}, u32[]{:S(2)}, u32[]{:S(2)}) %all-to-all-start) | async-done | bytes 2359328 | tf_op jit(solution)/shard_map/all_to_all | solution.py:316
  86.4 6.0 %refine.1 = bf16[4,24,1024]{2,1,0:T(8,128)(2,1)S(1)} custom-call(bf16[9216,128]{1,0:T(8,128)(2,1)S(1)} %bitcast.14, bf16[64,1024]{1,0:T(8,128)(2,1)S(1)} %dynamic-slice_bitcast_fusion.table_ref, f32[8,128]{1,0:T(8,128)S(1)} %stack.5.wave_ref, bf16[128,2048]{1,0:T(8,128)(2,1)S(1)} %and_convert_fusion.widen_ref), custom_call_target="tpu_custom_call" | custom-call | tf_op jit(solution)/shard_map/refine/pallas_call | solution.py:351
  92.3 8.0 %all_to_all.15.recv_ref = bf16[4,24,1024]{2,1,0:T(8,128)(2,1)S(1)} all-to-all(bf16[4,24,1024]{2,1,0:T(8,128)(2,1)S(1)} %refine.1), channel_id=1, replica_groups=mesh['cls'=128,'dp'=4] {'dp'}, dimensions={0} | all-to-all | bytes 393216 | tf_op jit(solution)/shard_map/all_to_all | solution.py:368
  100.3 0.6 spread.1
  100.9 9.6 %all-to-all-start.2 = ((f32[128,1,128]{2,1,0:T(1,128)}), f32[128,1,128]{2,1,0:T(1,128)S(1)}, u32[]{:S(2)}, u32[]{:S(2)}) async-start(f32[128,1,128]{2,1,0:T(1,128)} %bitcast.9), calls=%async_computation.2 | async-start | bytes 131072 | tf_op jit(solution)/shard_map/all_to_all | solution.py:377
  110.5 0.7 join.1
  111.2 10.9 %all-to-all-done.2 = f32[128,1,128]{2,1,0:T(1,128)S(1)} async-done(((f32[128,1,128]{2,1,0:T(1,128)}), f32[128,1,128]{2,1,0:T(1,128)S(1)}, u32[]{:S(2)}, u32[]{:S(2)}) %all-to-all-start.2) | async-done | bytes 65568 | tf_op jit(solution)/shard_map/all_to_all | solution.py:377
  122.1 0.0 copy-done.1
  122.1 0.6 settle.1
  (13 shorter events, 0.1 us)
Async XLA Ops:
  0.6 26.6 %copy-start = (bf16[1,64,4096]{2,1,0:T(8,128)(2,1)S(1)}, bf16[1,64,4096]{2,1,0:T(8,128)(2,1)}, u32[]{:S(2)}) copy-start(bf16[1,64,4096]{2,1,0:T(8,128)(2,1)} %param.9) | copy-start | bytes 1572868
  4.9 81.4 %all-to-all-start = ((bf16[4608,2,128]{2,1,0:T(2,128)(2,1)}), bf16[4608,2,128]{2,1,0:T(2,128)(2,1)S(1)}, u32[]{:S(2)}, u32[]{:S(2)}) async-start(bf16[4608,2,128]{2,1,0:T(2,128)(2,1)} %bitcast.16), calls=%async_computation | async-start | bytes 4718592 | tf_op jit(solution)/shard_map/all_to_all | solution.py:316
  27.3 94.8 %copy-start.1 = (s32[1,128]{1,0:T(1,128)S(1)}, s32[1,128]{1,0:T(1,128)}, u32[]{:S(2)}) copy-start(s32[1,128]{1,0:T(1,128)} %get-tuple-element.5.key_ref) | copy-start | bytes 1540
  100.9 21.2 %all-to-all-start.2 = ((f32[128,1,128]{2,1,0:T(1,128)}), f32[128,1,128]{2,1,0:T(1,128)S(1)}, u32[]{:S(2)}, u32[]{:S(2)}) async-start(f32[128,1,128]{2,1,0:T(1,128)} %bitcast.9), calls=%async_computation.2 | async-start | bytes 131072 | tf_op jit(solution)/shard_map/all_to_all | solution.py:377

commit v5 on v4

--- a/solution.py
+++ b/solution.py
@@ -26,14 +26,19 @@
 
 
 def pack_body(
+    class_hbm,
+    rotation_hbm,
+    defocus_hbm,
+    image_hbm,
+    out_hbm,
+    key_ref,
     class_ref,
     rotation_ref,
     defocus_ref,
     image_ref,
-    out_hbm,
-    key_ref,
     rows_ref,
     out_ref,
+    load_sems,
     store_sems,
 ):
     particles = image_ref.shape[0]
@@ -47,8 +52,18 @@
         rows = pl.ds(part * part_rows, part_rows)
         return pltpu.make_async_copy(out_ref.at[rows], out_hbm.at[rows], store_sems.at[part])
 
+    sources = (class_hbm, rotation_hbm, defocus_hbm, image_hbm)
+    targets = (class_ref, rotation_ref, defocus_ref, image_ref)
+    loads = [
+        pltpu.make_async_copy(source, target, load_sems.at[place])
+        for place, (source, target) in enumerate(zip(sources, targets))
+    ]
+    for load in loads:
+        load.start()
     parts = store_sems.shape[0]
     part_rows = out_ref.shape[0] // parts
+    for load in loads[:3]:
+        load.wait()
     class_row = jnp.broadcast_to(class_ref[...].astype(jnp.float32), (particles, particles))
     class_column = class_row.T
     down = lax.broadcasted_iota(jnp.int32, (particles, particles), 0)
@@ -68,6 +83,7 @@
             first = group * block + slot
             rows_ref[pl.ds(first + quarter * SLOTS, particles, stride=groups * block), :] = meta
         choosers.append(chosen.astype(jnp.bfloat16))
+    loads[3].wait()
     owners = particles // parts
     for part in range(parts):
         for group in range(groups):
@@ -103,8 +119,8 @@
     misfit_ref,
     table_next_ref,
 ):
-    rotations = table_ref.shape[0]
-    width = table_ref.shape[1]
+    rotations, width = table_ref.shape[0], out_ref.shape[2]
+    origin = lax.axis_index("dp") * width
     quarter = width // LANES
     block = SLOTS * (quarter + 1)
     sources = recv_ref.shape[0] // block
@@ -160,7 +176,11 @@
         wide = jnp.dot(
             rows.astype(jnp.bfloat16), widen_ref[...], preferred_element_type=jnp.float32
         )
-        tiles = jnp.dot(pick[:, :rotations], table_ref[...], preferred_element_type=jnp.float32)
+        tiles = jnp.dot(
+            pick[:, :rotations],
+            table_ref[:, pl.ds(pl.multiple_of(origin, width), width)],
+            preferred_element_type=jnp.float32,
+        )
         for tile in range(quarter):
             image = rows_ref[pl.ds(start + tile * SLOTS, step, stride=block), :]
             contrast = (
@@ -190,7 +210,8 @@
         gradient = summed[:, spot : spot + LANES]
         weight = summed[:, spot + LANES : spot + 256]
         lanes = slice(tile * LANES, (tile + 1) * LANES)
-        table = table_ref[:, lanes].astype(jnp.float32)
+        place = pl.multiple_of(origin + tile * LANES, LANES)
+        table = table_ref[:, pl.ds(place, LANES)].astype(jnp.float32)
         table_next = (table - gradient / damping).astype(jnp.bfloat16)
         table_next_ref[:, lanes] = table_next
         table_next = table_next.astype(jnp.float32)
@@ -299,11 +320,16 @@
             jax.ShapeDtypeStruct((message_rows, LANES), jnp.bfloat16),
             jax.ShapeDtypeStruct((1, particles), jnp.int32),
         ),
-        in_specs=[VMEM] * 4,
+        in_specs=[ANY] * 4,
         out_specs=(ANY, VMEM),
         scratch_shapes=[
+            pltpu.VMEM((1, particles), jnp.int32),
+            pltpu.VMEM((1, particles), jnp.int32),
+            pltpu.VMEM((1, particles), jnp.bfloat16),
+            pltpu.VMEM((particles, pixels), jnp.bfloat16),
             pltpu.VMEM((message_rows, LANES), jnp.float32),
             pltpu.VMEM((message_rows, LANES), jnp.bfloat16),
+            pltpu.SemaphoreType.DMA((4,)),
             pltpu.SemaphoreType.DMA((PARTS,)),
         ],
         name="pack",
@@ -347,7 +373,6 @@
     target = lax.broadcasted_iota(jnp.int32, (LANES, 2 * width), 1)
     wanted = target // LANES % 2 * held + target // (2 * LANES) * 2 + target % LANES // SIDE
     widen = ((source % (2 * held) == wanted) & (source < 6 * held)).astype(jnp.bfloat16)
-    table = lax.dynamic_slice_in_dim(references[0], group * width, width, 1)
     spread = pl.pallas_call(
         refine_body,
         out_shape=jax.ShapeDtypeStruct((count_dp, share + 8, width), jnp.bfloat16),
@@ -364,7 +389,7 @@
         ],
         compiler_params=pltpu.CompilerParams(vmem_limit_bytes=22 << 20),
         name="refine",
-    )(received, table, wave, widen)
+    )(received, references[0], wave, widen)
     turned = lax.all_to_all(spread, "dp", split_axis=0, concat_axis=0, tiled=True)
     returning = pl.pallas_call(
         spread_body,

time: 123 us -> 123 us (level)
  no operation moved by 1% of the time
where the time goes in v5:
time: 123 us; the launch traced here: 122 us
  waiting for transfers between devices  69.7 us (57%)
  starting transfers between devices  31.7 us (26%)
  Pallas kernels  11.9 us (10%)
  blocking collectives  7.95 us (6%)
    all_to_all x1, waiting for transfers between devices, shards(): lax.all_to_all(packed.reshape(message_rows // SLOTS, SLOTS, LANES), ('cls...  58.8 us
    all_to_all x1, starting transfers between devices, shards(): lax.all_to_all(packed.reshape(message_rows // SLOTS, SLOTS, LANES), ('cls...  22.2 us
    all_to_all x1, waiting for transfers between devices, shards(): lax.all_to_all(returning.reshape(count_cls, 1, LANES), 'cls', split_axis=...  10.9 us
    all_to_all x1, starting transfers between devices, shards(): lax.all_to_all(returning.reshape(count_cls, 1, LANES), 'cls', split_axis=...  9.57 us
    all_to_all x1, blocking collectives, shards(): lax.all_to_all(spread, 'dp', split_axis=0, concat_axis=0, tiled=True)  7.95 us
    pallas_call x1, Pallas kernels, shards(): pl.pallas_call(refine_body, out_shape=jax.ShapeDtypeStruct((count_dp, sha...  5.91 us
    pallas_call x1, Pallas kernels, shards(): pl.pallas_call(pack_body, out_shape=(jax.ShapeDtypeStruct((message_rows,...  4.09 us
  transfers between devices with their start and end apart: 2, of which 2 were waited for; matrix products, arithmetic and copies ran while one was open for 0% of the time, Pallas kernels for 1%

profile of v5, /device:TPU:1, one launch (start us, length us, event | category | flops | bytes accessed | tf_op | source)
XLA Modules:
  0.0 122.5 jit_solution(8819514983037516387)
XLA Ops:
  0.6 4.1 %pack.1 = (bf16[9216,128]{1,0:T(8,128)(2,1)}, s32[1,128]{1,0:T(1,128)}) custom-call(s32[1,128]{1,0:T(1,128)} %bitcast.18, s32[1,128]{1,0:T(1,128)} %bitcast.19, bf16[1,128]{1,0:T(2,128)(2,1)} %bitcast.20, bf16[128,4096]{1,0:T(8,128)(2,1)} %image_hbm.1), custom_call_target="tpu_custom_call" | custom-call | tf_op jit(solution)/shard_map/pack/pallas_call | solution.py:317
  4.7 0.0 copy-start
  4.7 22.2 %all-to-all-start = ((bf16[4608,2,128]{2,1,0:T(2,128)(2,1)}), bf16[4608,2,128]{2,1,0:T(2,128)(2,1)S(1)}, u32[]{:S(2)}, u32[]{:S(2)}) async-start(bf16[4608,2,128]{2,1,0:T(2,128)(2,1)} %bitcast.16), calls=%async_computation | async-start | bytes 4718592 | tf_op jit(solution)/shard_map/all_to_all | solution.py:342
  27.1 0.3 and_convert_fusion.widen_ref
  27.4 58.8 %all-to-all-done = bf16[4608,2,128]{2,1,0:T(2,128)(2,1)S(1)} async-done(((bf16[4608,2,128]{2,1,0:T(2,128)(2,1)}), bf16[4608,2,128]{2,1,0:T(2,128)(2,1)S(1)}, u32[]{:S(2)}, u32[]{:S(2)}) %all-to-all-start) | async-done | bytes 2359328 | tf_op jit(solution)/shard_map/all_to_all | solution.py:342
  86.2 0.0 copy-done
  86.2 0.0 copy-start.1
  86.2 5.9 %refine.1 = bf16[4,24,1024]{2,1,0:T(8,128)(2,1)S(1)} custom-call(bf16[9216,128]{1,0:T(8,128)(2,1)S(1)} %bitcast.13, bf16[64,4096]{1,0:T(8,128)(2,1)S(1)} %bitcast.14, f32[8,128]{1,0:T(8,128)S(1)} %stack.5.wave_ref, bf16[128,2048]{1,0:T(8,128)(2,1)S(1)} %and_convert_fusion.widen_ref), custom_call_target="tpu_custom_call" | custom-call | tf_op jit(solution)/shard_map/refine/pallas_call | solution.py:376
  92.1 8.0 %all_to_all.15.recv_ref = bf16[4,24,1024]{2,1,0:T(8,128)(2,1)S(1)} all-to-all(bf16[4,24,1024]{2,1,0:T(8,128)(2,1)S(1)} %refine.1), channel_id=1, replica_groups=mesh['cls'=128,'dp'=4] {'dp'}, dimensions={0} | all-to-all | bytes 393216 | tf_op jit(solution)/shard_map/all_to_all | solution.py:393
  100.1 0.6 spread.1
  100.7 9.6 %all-to-all-start.2 = ((f32[128,1,128]{2,1,0:T(1,128)}), f32[128,1,128]{2,1,0:T(1,128)S(1)}, u32[]{:S(2)}, u32[]{:S(2)}) async-start(f32[128,1,128]{2,1,0:T(1,128)} %bitcast.9), calls=%async_computation.2 | async-start | bytes 131072 | tf_op jit(solution)/shard_map/all_to_all | solution.py:402
  110.3 0.7 join.1
  110.9 10.9 %all-to-all-done.2 = f32[128,1,128]{2,1,0:T(1,128)S(1)} async-done(((f32[128,1,128]{2,1,0:T(1,128)}), f32[128,1,128]{2,1,0:T(1,128)S(1)}, u32[]{:S(2)}, u32[]{:S(2)}) %all-to-all-start.2) | async-done | bytes 65568 | tf_op jit(solution)/shard_map/all_to_all | solution.py:402
  121.8 0.0 copy-done.1
  121.8 0.6 settle.1
  (12 shorter events, 0.1 us)
Async XLA Ops:
  4.7 81.5 %copy-start = (bf16[1,64,4096]{2,1,0:T(8,128)(2,1)S(1)}, bf16[1,64,4096]{2,1,0:T(8,128)(2,1)}, u32[]{:S(2)}) copy-start(bf16[1,64,4096]{2,1,0:T(8,128)(2,1)} %param.9) | copy-start | bytes 1572868
  4.7 81.4 %all-to-all-start = ((bf16[4608,2,128]{2,1,0:T(2,128)(2,1)}), bf16[4608,2,128]{2,1,0:T(2,128)(2,1)S(1)}, u32[]{:S(2)}, u32[]{:S(2)}) async-start(bf16[4608,2,128]{2,1,0:T(2,128)(2,1)} %bitcast.16), calls=%async_computation | async-start | bytes 4718592 | tf_op jit(solution)/shard_map/all_to_all | solution.py:342
  86.2 35.7 %copy-start.1 = (s32[1,128]{1,0:T(1,128)S(1)}, s32[1,128]{1,0:T(1,128)}, u32[]{:S(2)}) copy-start(s32[1,128]{1,0:T(1,128)} %get-tuple-element.5.key_ref) | copy-start | bytes 1540
  100.7 21.2 %all-to-all-start.2 = ((f32[128,1,128]{2,1,0:T(1,128)}), f32[128,1,128]{2,1,0:T(1,128)S(1)}, u32[]{:S(2)}, u32[]{:S(2)}) async-start(f32[128,1,128]{2,1,0:T(1,128)} %bitcast.9), calls=%async_computation.2 | async-start | bytes 131072 | tf_op jit(solution)/shard_map/all_to_all | solution.py:402

commit v6 on v5

--- a/solution.py
+++ b/solution.py
@@ -119,7 +119,7 @@
     misfit_ref,
     table_next_ref,
 ):
-    rotations, width = table_ref.shape[0], out_ref.shape[2]
+    rotations, width = table_ref.shape[0], out_ref.shape[2] - LANES
     origin = lax.axis_index("dp") * width
     quarter = width // LANES
     block = SLOTS * (quarter + 1)
@@ -218,7 +218,7 @@
         gradient = gradient - weight * (table - table_next)
         refined = (table_next - gradient / damping).astype(jnp.bfloat16)
         for group in range(groups):
-            out_ref[group, :share, lanes] = refined[group * share : (group + 1) * share]
+            out_ref[group, :, lanes] = refined[group * share : (group + 1) * share]
 
     def second_pass(index, carry):
         slot, chunk = index // per_slot, index % per_slot
@@ -242,8 +242,8 @@
         return carry
 
     lax.fori_loop(0, particles // step, second_pass, 0, unroll=2)
-    ones = jnp.full((8, LANES), 1.0 / (groups * width), jnp.float32)
-    level = lax.broadcasted_iota(jnp.int32, (8, width), 0)
+    ones = jnp.ones((8, 2 * LANES), jnp.bfloat16)
+    level = lax.broadcasted_iota(jnp.int32, (8, LANES), 0)
     for group in range(groups):
         mine = jnp.concatenate(
             [
@@ -256,35 +256,39 @@
             ],
             axis=0,
         )
+        high = mine.astype(jnp.bfloat16)
+        low = (mine - high.astype(jnp.float32)).astype(jnp.bfloat16)
         mean = lax.dot_general(
             ones,
-            mine,
+            jnp.concatenate([high, low], axis=1),
             (((1,), (1,)), ((), ())),
-            precision=lax.Precision.HIGHEST,
             preferred_element_type=jnp.float32,
-        )
+        ) * (1.0 / (groups * width))
         high = mean.astype(jnp.bfloat16).astype(jnp.float32)
-        mean = jnp.where(level[:, : mean.shape[1]] == 0, high, mean - high)
-        out_ref[group, share:, : mean.shape[1]] = mean.astype(jnp.bfloat16)
-        out_ref[group, share:, mean.shape[1] :] = jnp.zeros(
-            (8, width - mean.shape[1]), jnp.bfloat16
-        )
+        low = mean - high
+        pieces = (high[:, :LANES], high[:, LANES:], low[:, :LANES], low[:, LANES:])
+        rows = jnp.zeros((8, LANES), jnp.float32)
+        for place, piece in enumerate(pieces):
+            rows = jnp.where(level == place, piece, rows)
+        out_ref[group, :8, width:] = rows.astype(jnp.bfloat16)
+        out_ref[group, 8:, width:] = jnp.zeros((share - 8, LANES), jnp.bfloat16)
 
 
 def spread_body(recv_ref, out_ref):
-    share = recv_ref.shape[1] - 8
     homes, lanes = out_ref.shape
-    total = jnp.sum(recv_ref[:, share:, : 2 * lanes].astype(jnp.float32), axis=0)
-    total = total[0:1] + total[1:2]
+    width = recv_ref.shape[2] - lanes
+    total = jnp.sum(recv_ref[:, :8, width:].astype(jnp.float32), axis=0)
     home = lax.broadcasted_iota(jnp.int32, out_ref.shape, 0)
-    out_ref[...] = jnp.where(home < homes // 2, total[:, :lanes], total[:, lanes:])
+    out_ref[...] = jnp.where(
+        home < homes // 2, total[0:1] + total[2:3], total[1:2] + total[3:4]
+    )
 
 
 def join_body(recv_ref, out_ref):
-    groups, share = recv_ref.shape[0], recv_ref.shape[1] - 8
-    width = recv_ref.shape[2]
+    groups = recv_ref.shape[0]
+    width = out_ref.shape[1] // groups
     for group in range(groups):
-        out_ref[:, group * width : (group + 1) * width] = recv_ref[group, :share, :]
+        out_ref[:, group * width : (group + 1) * width] = recv_ref[group, :, :width]
 
 
 def settle_body(own_ref, recv_ref, key_ref, out_ref):
@@ -375,7 +379,7 @@
     widen = ((source % (2 * held) == wanted) & (source < 6 * held)).astype(jnp.bfloat16)
     spread = pl.pallas_call(
         refine_body,
-        out_shape=jax.ShapeDtypeStruct((count_dp, share + 8, width), jnp.bfloat16),
+        out_shape=jax.ShapeDtypeStruct((count_dp, share, width + LANES), jnp.bfloat16),
         in_specs=[VMEM] * 4,
         out_specs=VMEM,
         scratch_shapes=[

time: 123 us -> 122 us (level)
  no operation moved by 1% of the time
where the time goes in v6:
time: 122 us
  waiting for transfers between devices  69.7 us (57%)
  starting transfers between devices  31.7 us (26%)
  Pallas kernels  11.7 us (10%)
  blocking collectives  7.69 us (6%)
    all_to_all x1, waiting for transfers between devices, shards(): lax.all_to_all(packed.reshape(message_rows // SLOTS, SLOTS, LANES), ('cls...  58.8 us
    all_to_all x1, starting transfers between devices, shards(): lax.all_to_all(packed.reshape(message_rows // SLOTS, SLOTS, LANES), ('cls...  22.2 us
    all_to_all x1, waiting for transfers between devices, shards(): lax.all_to_all(returning.reshape(count_cls, 1, LANES), 'cls', split_axis=...  10.9 us
    all_to_all x1, starting transfers between devices, shards(): lax.all_to_all(returning.reshape(count_cls, 1, LANES), 'cls', split_axis=...  9.57 us
    all_to_all x1, blocking collectives, shards(): lax.all_to_all(spread, 'dp', split_axis=0, concat_axis=0, tiled=True)  7.69 us
    pallas_call x1, Pallas kernels, shards(): pl.pallas_call(refine_body, out_shape=jax.ShapeDtypeStruct((count_dp, sha...  5.64 us
    pallas_call x1, Pallas kernels, shards(): pl.pallas_call(pack_body, out_shape=(jax.ShapeDtypeStruct((message_rows,...  4.09 us
  transfers between devices with their start and end apart: 2, of which 2 were waited for; matrix products, arithmetic and copies ran while one was open for 0% of the time, Pallas kernels for 1%

profile of v6, /device:TPU:1, one launch (start us, length us, event | category | flops | bytes accessed | tf_op | source)
XLA Modules:
  0.0 121.9 jit_solution(11556471490426064967)
XLA Ops:
  0.6 4.1 %pack.1 = (bf16[9216,128]{1,0:T(8,128)(2,1)}, s32[1,128]{1,0:T(1,128)}) custom-call(s32[1,128]{1,0:T(1,128)} %bitcast.18, s32[1,128]{1,0:T(1,128)} %bitcast.19, bf16[1,128]{1,0:T(2,128)(2,1)} %bitcast.20, bf16[128,4096]{1,0:T(8,128)(2,1)} %image_hbm.1), custom_call_target="tpu_custom_call" | custom-call | tf_op jit(solution)/shard_map/pack/pallas_call | solution.py:321
  4.7 0.0 copy-start
  4.7 22.2 %all-to-all-start = ((bf16[4608,2,128]{2,1,0:T(2,128)(2,1)}), bf16[4608,2,128]{2,1,0:T(2,128)(2,1)S(1)}, u32[]{:S(2)}, u32[]{:S(2)}) async-start(bf16[4608,2,128]{2,1,0:T(2,128)(2,1)} %bitcast.16), calls=%async_computation | async-start | bytes 4718592 | tf_op jit(solution)/shard_map/all_to_all | solution.py:346
  27.1 0.3 and_convert_fusion.widen_ref
  27.4 0.0 copy-start.1
  27.4 58.8 %all-to-all-done = bf16[4608,2,128]{2,1,0:T(2,128)(2,1)S(1)} async-done(((bf16[4608,2,128]{2,1,0:T(2,128)(2,1)}), bf16[4608,2,128]{2,1,0:T(2,128)(2,1)S(1)}, u32[]{:S(2)}, u32[]{:S(2)}) %all-to-all-start) | async-done | bytes 2359328 | tf_op jit(solution)/shard_map/all_to_all | solution.py:346
  86.2 0.0 copy-done
  86.2 5.6 %refine.1 = bf16[4,16,1152]{2,1,0:T(8,128)(2,1)S(1)} custom-call(bf16[9216,128]{1,0:T(8,128)(2,1)S(1)} %bitcast.13, bf16[64,4096]{1,0:T(8,128)(2,1)S(1)} %bitcast.14, f32[8,128]{1,0:T(8,128)S(1)} %stack.5.wave_ref, bf16[128,2048]{1,0:T(8,128)(2,1)S(1)} %and_convert_fusion.widen_ref), custom_call_target="tpu_custom_call" | custom-call | tf_op jit(solution)/shard_map/refine/pallas_call | solution.py:380
  91.8 7.7 %all_to_all.15.recv_ref = bf16[4,16,1152]{2,1,0:T(8,128)(2,1)S(1)} all-to-all(bf16[4,16,1152]{2,1,0:T(8,128)(2,1)S(1)} %refine.1), channel_id=1, replica_groups=mesh['cls'=128,'dp'=4] {'dp'}, dimensions={0} | all-to-all | bytes 294912 | tf_op jit(solution)/shard_map/all_to_all | solution.py:397
  99.5 0.6 spread.1
  100.1 9.6 %all-to-all-start.2 = ((f32[128,1,128]{2,1,0:T(1,128)}), f32[128,1,128]{2,1,0:T(1,128)S(1)}, u32[]{:S(2)}, u32[]{:S(2)}) async-start(f32[128,1,128]{2,1,0:T(1,128)} %bitcast.9), calls=%async_computation.2 | async-start | bytes 131072 | tf_op jit(solution)/shard_map/all_to_all | solution.py:406
  109.7 0.7 join.1
  110.4 10.9 %all-to-all-done.2 = f32[128,1,128]{2,1,0:T(1,128)S(1)} async-done(((f32[128,1,128]{2,1,0:T(1,128)}), f32[128,1,128]{2,1,0:T(1,128)S(1)}, u32[]{:S(2)}, u32[]{:S(2)}) %all-to-all-start.2) | async-done | bytes 65568 | tf_op jit(solution)/shard_map/all_to_all | solution.py:406
  121.3 0.0 copy-done.1
  121.3 0.6 settle.1
  (12 shorter events, 0.1 us)
Async XLA Ops:
  4.7 81.5 %copy-start = (bf16[1,64,4096]{2,1,0:T(8,128)(2,1)S(1)}, bf16[1,64,4096]{2,1,0:T(8,128)(2,1)}, u32[]{:S(2)}) copy-start(bf16[1,64,4096]{2,1,0:T(8,128)(2,1)} %param.9) | copy-start | bytes 1572868
  4.7 81.4 %all-to-all-start = ((bf16[4608,2,128]{2,1,0:T(2,128)(2,1)}), bf16[4608,2,128]{2,1,0:T(2,128)(2,1)S(1)}, u32[]{:S(2)}, u32[]{:S(2)}) async-start(bf16[4608,2,128]{2,1,0:T(2,128)(2,1)} %bitcast.16), calls=%async_computation | async-start | bytes 4718592 | tf_op jit(solution)/shard_map/all_to_all | solution.py:346
  27.4 93.9 %copy-start.1 = (s32[1,128]{1,0:T(1,128)S(1)}, s32[1,128]{1,0:T(1,128)}, u32[]{:S(2)}) copy-start(s32[1,128]{1,0:T(1,128)} %get-tuple-element.5.key_ref) | copy-start | bytes 1540
  100.1 21.1 %all-to-all-start.2 = ((f32[128,1,128]{2,1,0:T(1,128)}), f32[128,1,128]{2,1,0:T(1,128)S(1)}, u32[]{:S(2)}, u32[]{:S(2)}) async-start(f32[128,1,128]{2,1,0:T(1,128)} %bitcast.9), calls=%async_computation.2 | async-start | bytes 131072 | tf_op jit(solution)/shard_map/all_to_all | solution.py:406
